TPU v7x, 256 devices: a whole 4x4x8 slice. The times are simulated.
256 devices in a mesh: expert: 32 (over y, x, core), dp: 8 (over z).
Axes of the slice: x: 4, y: 4, z: 8, core: 2. Of those that a mesh axis runs over, the one named last changes fastest.
Arguments:
- tokens: bfloat16 [32768, 2048], P(('expert', 'dp')), may hold values from -6 to 6
- cotangent: bfloat16 [32768, 2048], P(('expert', 'dp')), may hold values from -6 to 6
- routes: int32 [32768, 4], P(('expert', 'dp')), may hold values from 0 to 31, all different within a row; in each aligned block of 128 rows (0 to 127, 128 to 255, ...) at most 24 rows name the same one
- gate_values: bfloat16 [32768, 4], P(('expert', 'dp')), may hold values from 0.099609375 to 1
- w_gate: bfloat16 [32, 2048, 512], P('expert', 'dp'), may hold values from -0.125 to 0.125
- w_up: bfloat16 [32, 2048, 512], P('expert', 'dp'), may hold values from -0.125 to 0.125
- w_down: bfloat16 [32, 512, 2048], P('expert', None, 'dp'), may hold values from -0.25 to 0.25
Outputs:
- token_grad: bfloat16 [32768, 2048], P(('expert', 'dp'))
- gate_weight_grad: bfloat16 [32, 2048, 512], P('expert', 'dp')
- up_weight_grad: bfloat16 [32, 2048, 512], P('expert', 'dp')
- down_weight_grad: bfloat16 [32, 512, 2048], P('expert', None, 'dp')
Inputs may be any that keep to these rules, and one draw needn't show every extreme that they name: `routes`: each row names 4 different experts. Among the rows of one device no expert is named more than 24 times, and some device names some expert exactly 24 times.
All inputs are finite; a program needn't handle non-finite values.
Results may differ from a plain program's by a relative error of at most 0.017.
Values may be sent and summed in bfloat16 or wider, within the bound.
No kernel may reach another device: no remote copies, remote signals or barrier semaphores. Data moves between devices by JAX's collectives and lax.ppermute only.
A program may use at most 128 MiB of HBM per device.

v0:
```python
import jax
import jax.numpy as jnp
from jax import lax
from jax.experimental import pallas as pl
from jax.experimental.pallas import tpu as pltpu
from jax.sharding import PartitionSpec as P

ROWS = 384
COLS = 256
TERM_COLS = 512
PACK_COLS = 512


def matmul(a, b, dims=((1,), (0,))):
    return lax.dot_general(a, b, (dims, ((), ())), preferred_element_type=jnp.float32)


def pack_kernel(
    capacity,
    routes_ref,
    gate_ref,
    tokens_hbm,
    cotangent_hbm,
    w_gate_hbm,
    w_up_hbm,
    w_down_hbm,
    packed_hbm,
    rank_ref,
    shard_a_hbm,
    shard_b_hbm,
    tokens,
    shards,
    down,
    place,
    packed,
    in_sems,
    w_sems,
    shard_sems,
    out_sems,
):
    experts, tok_dev = rank_ref.shape
    width = tokens_hbm.shape[1]
    sources = [tokens_hbm, cotangent_hbm]
    row_copies = [
        pltpu.make_async_copy(sources[k], tokens.at[k], in_sems.at[k]) for k in range(2)
    ]
    w_copies = [
        pltpu.make_async_copy(w_gate_hbm.at[0], shards.at[0], w_sems.at[0]),
        pltpu.make_async_copy(w_up_hbm.at[0], shards.at[1], w_sems.at[1]),
        pltpu.make_async_copy(w_down_hbm.at[0], down, w_sems.at[2]),
    ]
    for copy in row_copies + w_copies:
        copy.start()

    ids = lax.broadcasted_iota(jnp.int32, (experts, tok_dev), 0)
    gates = gate_ref[...].astype(jnp.float32)
    member = jnp.zeros((experts, tok_dev), jnp.float32)
    gate = jnp.zeros((experts, tok_dev), jnp.float32)
    for k in range(routes_ref.shape[0]):
        hit = routes_ref[k : k + 1, :] == ids
        member = jnp.where(hit, 1.0, member)
        gate = jnp.where(hit, gates[k : k + 1, :], gate)
    row = lax.broadcasted_iota(jnp.int32, (tok_dev, tok_dev), 0)
    col = lax.broadcasted_iota(jnp.int32, (tok_dev, tok_dev), 1)
    before = matmul(member.astype(jnp.bfloat16), (row < col).astype(jnp.bfloat16))
    rank = jnp.where(member > 0.5, before, -1.0)
    rank_ref[...] = rank.astype(jnp.int32)
    slots = lax.broadcasted_iota(jnp.int32, (capacity, tok_dev), 0).astype(jnp.float32)
    for e in range(0, experts, 2):
        here, gate_here = [], []
        for f in (e, e + 1):
            mask = jnp.broadcast_to(rank[f : f + 1, :], (capacity, tok_dev)) == slots
            here.append(jnp.where(mask, 1.0, 0.0))
            gate_here.append(
                jnp.where(mask, jnp.broadcast_to(gate[f : f + 1, :], (capacity, tok_dev)), 0.0)
            )
        span = slice(e * capacity, (e + 2) * capacity)
        place[0, span, :] = jnp.concatenate(here, axis=0).astype(place.dtype)
        place[1, span, :] = jnp.concatenate(gate_here, axis=0).astype(place.dtype)

    half = shards.shape[1] // 2
    shard_copies = [
        [
            pltpu.make_async_copy(
                shards.at[k, pl.ds(c * half, half), :],
                out.at[pl.ds(k * half, half), :],
                shard_sems.at[k, c],
            )
            for c, out in enumerate((shard_a_hbm, shard_b_hbm))
        ]
        for k in range(3)
    ]
    steps = width // PACK_COLS

    def out_copy(i):
        cols = (slice(None), pl.ds(pl.multiple_of(i * PACK_COLS, PACK_COLS), PACK_COLS))
        return pltpu.make_async_copy(packed.at[cols], packed_hbm.at[cols], out_sems.at[i])

    for k in range(2):
        row_copies[k].wait()

        @pl.loop(0, steps)
        def _(i):
            source = pl.ds(pl.multiple_of(i * PACK_COLS, PACK_COLS), PACK_COLS)
            target = pl.ds(pl.multiple_of((k * steps + i) * PACK_COLS, PACK_COLS), PACK_COLS)
            packed[:, target] = matmul(place[k], tokens[k, :, source]).astype(packed.dtype)
            out_copy(k * steps + i).start()

        if k == 0:
            for m in range(3):
                w_copies[m].wait()
                if m == 2:
                    shards[2] = down[...].T
                for copy in shard_copies[m]:
                    copy.start()
    for copy in sum(shard_copies, [out_copy(i) for i in range(2 * steps)]):
        copy.wait()


def pack(routes, gate_values, tokens, cotangent, w_gate, w_up, w_down, experts, capacity):
    tok_dev, width = tokens.shape
    slots = experts * capacity
    vmem = pl.BlockSpec(memory_space=pltpu.VMEM)
    hbm = pl.BlockSpec(memory_space=pl.ANY)
    return pl.pallas_call(
        lambda *refs: pack_kernel(capacity, *refs),
        in_specs=[vmem] * 2 + [hbm] * 5,
        out_specs=[hbm, vmem, hbm, hbm],
        out_shape=[
            jax.ShapeDtypeStruct((slots, 2 * width), tokens.dtype),
            jax.ShapeDtypeStruct((experts, tok_dev), jnp.int32),
            *[jax.ShapeDtypeStruct((3 * w_gate.shape[1] // 2, w_gate.shape[2]), w_gate.dtype)] * 2,
        ],
        scratch_shapes=[
            pltpu.VMEM((2, tok_dev, width), tokens.dtype),
            pltpu.VMEM((3, *w_gate.shape[1:]), w_gate.dtype),
            pltpu.VMEM(w_down.shape[1:], w_down.dtype),
            pltpu.VMEM((2, slots, tok_dev), jnp.bfloat16),
            pltpu.VMEM((slots, 2 * width), tokens.dtype),
            pltpu.SemaphoreType.DMA((2,)),
            pltpu.SemaphoreType.DMA((3,)),
            pltpu.SemaphoreType.DMA((3, 2)),
            pltpu.SemaphoreType.DMA((2 * width // PACK_COLS,)),
        ],
        compiler_params=pltpu.CompilerParams(vmem_limit_bytes=60 << 20),
        cost_estimate=pl.CostEstimate(
            flops=4 * slots * tok_dev * width,
            bytes_accessed=4 * slots * width,
            transcendentals=0,
        ),
        name="pack",
    )(routes.T, gate_values.T, tokens, cotangent, w_gate, w_up, w_down)


def first_hops(n):
    far, near = n // 2, (n - 1) // 2
    return (far, near), (n - near, n - far)


def later_hops(n):
    sent = {(k, c) for pair in first_hops(n) for c, k in enumerate(pair)}
    return [(k, c) for k in range(n) for c in range(2) if (k, c) not in sent]


def block_terms(k, chains, me, parts, rows, grads, hidden_t, store):
    width = rows.shape[1] // 2
    ff = hidden_t.shape[0]
    block = width // parts
    half = block // 2
    start = lax.rem(me + k, parts) * block
    if len(chains) == 2:
        x_cols = rows[:, pl.ds(pl.multiple_of(start, block), block)]
    else:
        x_cols = rows[:, pl.ds(pl.multiple_of(start + chains[0] * half, half), half)]
    s_cols = rows[:, pl.ds(pl.multiple_of(width + start, block), block)]
    both = matmul(x_cols, grads[...], ((0,), (0,))).astype(jnp.bfloat16)
    if len(chains) == 2:
        down = matmul(hidden_t[...], s_cols).astype(jnp.bfloat16)
    for i, c in enumerate(chains):
        span = slice(i * half, (i + 1) * half)
        store(c, slice(0, half), slice(0, ff), both[span, :ff])
        store(c, slice(half, 2 * half), slice(0, ff), both[span, ff:])
        for h in range(ff // block):
            feature = slice(h * block + c * half, h * block + (c + 1) * half)
            if len(chains) == 2:
                value = down[feature]
            else:
                value = matmul(hidden_t[feature, :], s_cols).astype(jnp.bfloat16)
            store(c, slice(2 * half, 3 * half), slice(h * block, (h + 1) * block), value)


def terms_kernel(parts, me_ref, rows_hbm, *refs):
    pieces, refs = refs[: 2 * parts], refs[2 * parts :]
    grads_hbm, hidden_hbm, w_hbm, refs = refs[0], refs[1], refs[2], refs[3:]
    firsts, refs = refs[:2], refs[2:]
    rows, w, grads, hidden_t, terms, row_sems, w_sems, keep_sems, out_sems = refs
    _, width, ff = w.shape
    n = rows.shape[0]
    block = width // parts
    half = block // 2
    me = me_ref[0]

    def row_copy(k, left, size):
        span = (pl.ds(k * ROWS, ROWS), pl.ds(left, size))
        return pltpu.make_async_copy(
            rows_hbm.at[span], rows.at[span], row_sems.at[k + (1 if left else 0) + (k > 0)]
        )

    def w_copy(m, k, c):
        start = pl.multiple_of(lax.rem(me + parts - k, parts) * block + c * half, half)
        return pltpu.make_async_copy(
            pieces[2 * k + c].at[pl.ds(m * half, half), :],
            w.at[m, pl.ds(start, half), :],
            w_sems.at[m, k, c],
        )

    x_copy = row_copy(0, 0, width)
    scaled_copy = row_copy(0, width, width)
    later = [row_copy(k, 0, 2 * width) for k in range(1, n // ROWS)]
    w_copies = [[w_copy(m, k, c) for k in range(parts) for c in range(2)] for m in range(3)]
    for copy in [x_copy, *w_copies[0], *w_copies[1], scaled_copy, *w_copies[2], *later]:
        copy.start()
    keep = [
        pltpu.make_async_copy(grads, grads_hbm, keep_sems.at[0]),
        pltpu.make_async_copy(hidden_t, hidden_hbm, keep_sems.at[1]),
        pltpu.make_async_copy(w.at[pl.ds(0, 2)], w_hbm, keep_sems.at[2]),
    ]

    for k in range(n // ROWS):
        span = slice(k * ROWS, (k + 1) * ROWS)
        if k == 0:
            x_copy.wait()
            for copy in w_copies[0]:
                copy.wait()
        else:
            later[k - 1].wait()
        x = rows[span, :width]
        gate_pre = matmul(x, w[0])
        sig = 1.0 / (1.0 + jnp.exp(-gate_pre))
        activated = gate_pre * sig
        slope = sig * (1.0 + gate_pre * (1.0 - sig))
        if k == 0:
            for copy in w_copies[1]:
                copy.wait()
        up_pre = matmul(x, w[1])
        hidden_t[:, span] = (activated * up_pre).astype(jnp.bfloat16).T
        if k == 0:
            scaled_copy.wait()
            for copy in w_copies[2]:
                copy.wait()
        hidden_grad = matmul(rows[span, width:], w[2])
        grads[span, :ff] = (hidden_grad * up_pre * slope).astype(jnp.bfloat16)
        grads[span, ff:] = (hidden_grad * activated).astype(jnp.bfloat16)
        if k == 0:
            keep[2].start()

    keep[0].start()
    keep[1].start()
    hops = first_hops(parts)
    wanted = {}
    for d, pair in enumerate(hops):
        for c, k in enumerate(pair):
            wanted.setdefault(k, {})[c] = d
    for k, chains in wanted.items():

        def store(c, r, f, value):
            terms[chains[c], c * 3 * half + r.start : c * 3 * half + r.stop, f] = value

        block_terms(k, sorted(chains), me, parts, rows, grads, hidden_t, store)
    out_copies = [pltpu.make_async_copy(terms.at[d], firsts[d], out_sems.at[d]) for d in range(2)]
    for copy in out_copies:
        copy.start()
    for copy in [*keep, *out_copies]:
        copy.wait()


def terms_of(me, received, pieces):
    rows, width2 = received.shape
    width = width2 // 2
    parts = len(pieces) // 2
    piece_rows, ff = pieces[0].shape
    hbm = pl.BlockSpec(memory_space=pl.ANY)
    grads, hidden_t, w_in, *first = pl.pallas_call(
        lambda *refs: terms_kernel(parts, *refs),
        in_specs=[pl.BlockSpec(memory_space=pltpu.SMEM)] + [hbm] * (1 + 2 * parts),
        out_specs=[hbm] * 5,
        out_shape=[
            jax.ShapeDtypeStruct((rows, 2 * ff), jnp.bfloat16),
            jax.ShapeDtypeStruct((ff, rows), jnp.bfloat16),
            jax.ShapeDtypeStruct((2, width, ff), jnp.bfloat16),
            *[jax.ShapeDtypeStruct((2 * piece_rows, ff), jnp.bfloat16)] * 2,
        ],
        scratch_shapes=[
            pltpu.VMEM((rows, width2), jnp.bfloat16),
            pltpu.VMEM((3, width, ff), jnp.bfloat16),
            pltpu.VMEM((rows, 2 * ff), jnp.bfloat16),
            pltpu.VMEM((ff, rows), jnp.bfloat16),
            pltpu.VMEM((2, 2 * piece_rows, ff), jnp.bfloat16),
            pltpu.SemaphoreType.DMA((1 + rows // ROWS,)),
            pltpu.SemaphoreType.DMA((3, parts, 2)),
            pltpu.SemaphoreType.DMA((3,)),
            pltpu.SemaphoreType.DMA((2,)),
        ],
        compiler_params=pltpu.CompilerParams(vmem_limit_bytes=60 << 20),
        cost_estimate=pl.CostEstimate(
            flops=8 * rows * width * ff,
            bytes_accessed=2 * (2 * rows * width + 6 * width * ff),
            transcendentals=rows * ff,
        ),
        name="terms",
    )(me, received, *pieces)
    row_grad, *own = pl.pallas_call(
        lambda *refs: rest_kernel(parts, *refs),
        in_specs=[pl.BlockSpec(memory_space=pltpu.SMEM)] + [hbm] * 4,
        out_specs=[hbm] * (1 + len(later_hops(parts))),
        out_shape=[
            jax.ShapeDtypeStruct((rows, width), jnp.bfloat16),
            *[jax.ShapeDtypeStruct((piece_rows, ff), jnp.bfloat16)] * len(later_hops(parts)),
        ],
        scratch_shapes=[
            pltpu.VMEM((rows, width2), jnp.bfloat16),
            pltpu.VMEM((2, width, ff), jnp.bfloat16),
            pltpu.VMEM((rows, 2 * ff), jnp.bfloat16),
            pltpu.VMEM((ff, rows), jnp.bfloat16),
            pltpu.VMEM((rows, width), jnp.bfloat16),
            pltpu.VMEM((parts, 2, piece_rows, ff), jnp.bfloat16),
            pltpu.SemaphoreType.DMA((4,)),
            pltpu.SemaphoreType.DMA((width // TERM_COLS,)),
            pltpu.SemaphoreType.DMA((parts, 2)),
        ],
        compiler_params=pltpu.CompilerParams(vmem_limit_bytes=60 << 20),
        cost_estimate=pl.CostEstimate(
            flops=8 * rows * width * ff,
            bytes_accessed=2 * (3 * rows * width + 5 * width * ff),
            transcendentals=0,
        ),
        name="rest",
    )(me, received, grads, hidden_t, w_in)
    return row_grad, dict(zip(later_hops(parts), own)), first


def rest_kernel(parts, me_ref, rows_hbm, grads_hbm, hidden_hbm, w_hbm, row_grad_hbm, *refs):
    later = later_hops(parts)
    outs, refs = refs[: len(later)], refs[len(later) :]
    rows, w, grads, hidden_t, row_grad, terms, in_sems, row_sems, out_sems = refs
    _, width, ff = w.shape
    me = me_ref[0]
    sources = [grads_hbm, w_hbm, hidden_hbm, rows_hbm]
    targets = [grads, w, hidden_t, rows]
    arrive = [
        pltpu.make_async_copy(a, b, in_sems.at[k]) for k, (a, b) in enumerate(zip(sources, targets))
    ]
    for copy in arrive:
        copy.start()
    arrive[0].wait()
    arrive[1].wait()
    leave = []
    def row_copy(i):
        cols = (slice(None), pl.ds(pl.multiple_of(i * TERM_COLS, TERM_COLS), TERM_COLS))
        return pltpu.make_async_copy(row_grad.at[cols], row_grad_hbm.at[cols], row_sems.at[i])

    @pl.loop(0, width // TERM_COLS)
    def _(i):
        span = pl.ds(pl.multiple_of(i * TERM_COLS, TERM_COLS), TERM_COLS)
        value = matmul(grads[:, :ff], w[0, span, :], ((1,), (1,)))
        value = value + matmul(grads[:, ff:], w[1, span, :], ((1,), (1,)))
        row_grad[:, span] = value.astype(jnp.bfloat16)
        row_copy(i).start()

    leave += [row_copy(i) for i in range(width // TERM_COLS)]
    arrive[2].wait()
    arrive[3].wait()
    out_copies = {
        (k, c): pltpu.make_async_copy(terms.at[k, c], out, out_sems.at[k, c])
        for (k, c), out in zip(later, outs)
    }
    whole = [k for k in range(parts) if (k, 0) in later and (k, 1) in later]
    first = parts - (parts - 1) // 2 + 1

    def fill(k, chains):
        def store(c, r, f, value):
            terms[k, c, r, f] = value

        block_terms(k, chains, me, parts, rows, grads, hidden_t, store)

    for k, c in later:
        if k not in whole:
            fill(k, [c])
            out_copies[k, c].start()

    @pl.loop(0, len(whole))
    def _(i):
        k = lax.rem(first + i, parts)
        fill(k, [0, 1])
        for j in whole:

            @pl.when(k == j)
            def _():
                out_copies[j, 0].start()
                out_copies[j, 1].start()

    leave += list(out_copies.values())
    for copy in leave:
        copy.wait()


def finish_kernel(own_a, right_a, left_a, own_b, right_b, left_b, gate_ref, up_ref, down_ref):
    half = own_a.shape[0] // 3
    block = 2 * half
    for c, (own, right, left) in enumerate(((own_a, right_a, left_a), (own_b, right_b, left_b))):
        total = (
            own[...].astype(jnp.float32)
            + right[...].astype(jnp.float32)
            + left[...].astype(jnp.float32)
        ).astype(gate_ref.dtype)
        span = slice(c * half, (c + 1) * half)
        gate_ref[0, span, :] = total[:half]
        up_ref[0, span, :] = total[half : 2 * half]
        for h in range(total.shape[1] // block):
            down_ref[0, h * block + c * half : h * block + (c + 1) * half, :] = total[
                2 * half :, h * block : (h + 1) * block
            ]


def finish(*parts):
    piece_rows, ff = parts[0].shape
    rows = 2 * piece_rows // 3
    vmem = pl.BlockSpec(memory_space=pltpu.VMEM)
    return pl.pallas_call(
        finish_kernel,
        in_specs=[vmem] * 6,
        out_specs=[vmem] * 3,
        out_shape=[
            jax.ShapeDtypeStruct((1, rows, ff), parts[0].dtype),
            jax.ShapeDtypeStruct((1, rows, ff), parts[0].dtype),
            jax.ShapeDtypeStruct((1, ff, rows), parts[0].dtype),
        ],
        compiler_params=pltpu.CompilerParams(vmem_limit_bytes=60 << 20),
        name="finish",
    )(*parts)


def shift(a, by):
    n = lax.axis_size("dp")
    return lax.ppermute(a, "dp", [(i, (i + by) % n) for i in range(n)])


def ring_gather(shard, far):
    n = lax.axis_size("dp")
    moved = {1: [shard], -1: [shard]}
    for by in (far, -far):
        for _ in range(n // 2 if by == far else (n - 1) // 2):
            moved[by].append(shift(moved[by][-1], by))
    right, left = moved[1], moved[-1]
    return [right[k] if k < len(right) else left[n - k] for k in range(n)]


def ring_scatter(own, first, n):
    half = first[0].shape[0] // 2
    arrived = {
        (c, by): a[c * half : (c + 1) * half]
        for a, by in zip(first, (1, -1))
        for c in range(2)
    }
    left = {
        (c, by): hops[c] if by > 0 else n - hops[c]
        for hops, by in zip(first_hops(n), (1, -1))
        for c in range(2)
    }
    for _ in range(n // 2):
        for c in range(2):
            going = [by for by in (1, -1) if left[c, by] > 1]
            for by in going:
                left[c, by] -= 1
                mine = own[by * left[c, by] % n, c].astype(jnp.float32)
                total = arrived[c, by].astype(jnp.float32) + mine
                arrived[c, by] = shift(total.astype(jnp.bfloat16), by)
            if len(going) == 2:
                arrived[c, 1], arrived[c, -1] = lax.optimization_barrier(
                    (arrived[c, 1], arrived[c, -1])
                )
    return [a for c in range(2) for a in (own[0, c], arrived[c, 1], arrived[c, -1])]


def local(tokens, cotangent, routes, gate_values, w_gate, w_up, w_down):
    experts = lax.axis_size("expert")
    tok_dev, model_width = tokens.shape
    fan_out = routes.shape[1]
    capacity = min(tok_dev, 3 * tok_dev * fan_out // (2 * experts))

    def exchange(rows):
        return lax.all_to_all(
            rows.reshape(experts, capacity, rows.shape[1]),
            "expert",
            split_axis=0,
            concat_axis=0,
            tiled=True,
        ).reshape(rows.shape)

    packed, rank, shard_a, shard_b = pack(
        routes, gate_values, tokens, cotangent, w_gate, w_up, w_down, experts, capacity
    )
    received = exchange(packed)
    pieces_a, pieces_b = ring_gather(shard_a, 1), ring_gather(shard_b, -1)
    pieces = [p for pair in zip(pieces_a, pieces_b) for p in pair]
    me = lax.axis_index("dp").astype(jnp.int32).reshape(1)
    row_grad, own, first = terms_of(me, received, pieces)
    hops = [shift(a, by) for a, by in zip(first, (1, -1))]
    hops = lax.optimization_barrier(hops)
    sums = ring_scatter(own, hops, lax.axis_size("dp"))

    returned = exchange(row_grad)
    place = rank[:, None, :] == jnp.arange(capacity, dtype=jnp.int32)[None, :, None]
    place = place.reshape(experts * capacity, tok_dev).astype(jnp.bfloat16)
    token_grad = matmul(place, returned, ((0,), (0,))).astype(jnp.bfloat16)
    return (token_grad, *finish(*sums))


def solution(mesh):
    in_specs = (
        P(("expert", "dp"), None),
        P(("expert", "dp"), None),
        P(("expert", "dp"), None),
        P(("expert", "dp"), None),
        P("expert", "dp", None),
        P("expert", "dp", None),
        P("expert", None, "dp"),
    )
    out_specs = (
        P(("expert", "dp"), None),
        P("expert", "dp", None),
        P("expert", "dp", None),
        P("expert", None, "dp"),
    )
    return jax.shard_map(local, mesh=mesh, in_specs=in_specs, out_specs=out_specs, check_vma=False)
```

profile of v0, /device:TPU:2, one launch (start us, length us, event | category | flops | bytes accessed | tf_op | source)
XLA Modules:
  0.0 188.2 jit_solution(6357380809405950329)
XLA Ops:
  0.6 6.5 %pack.1 = (bf16[768,4096]{1,0:T(8,128)(2,1)}, s32[32,128]{1,0:T(8,128)}, bf16[384,512]{1,0:T(8,128)(2,1)}, bf16[384,512]{1,0:T(8,128)(2,1)}) custom-call(s32[4,128]{1,0:T(4,128)} %bitcast.12, bf16[4,128]{1,0:T(4,128)(2,1)} %bitcast.13, bf16[128,2048]{1,0:T(8,128)(2,1)} %refs_2_.1, bf16[128,2048]{1,0:T(8,128)(2,1)} %refs_3_.1, bf16[1,256,512]{2,1,0:T(8,128)(2,1)} %refs_4_.1, ...), custom_call_target="tpu_custom_call" | custom-call | flops 805306368 | bytes 6291456 | tf_op jit(solution)/shard_map/pack/pallas_call | solution.py:125
  7.1 7.8 %all-to-all-start = ((bf16[32,24,4096]{2,1,0:T(8,128)(2,1)}), bf16[32,24,4096]{2,1,0:T(8,128)(2,1)}, u32[]{:S(2)}, u32[]{:S(2)}) async-start(bf16[32,24,4096]{2,1,0:T(8,128)(2,1)} %bitcast.10), calls=%async_computation | async-start | bytes 12582912 | tf_op jit(solution)/shard_map/all_to_all | solution.py:492
  17.0 4.0 %collective-permute-start.7 = (bf16[384,512]{1,0:T(8,128)(2,1)S(1)}, bf16[384,512]{1,0:T(8,128)(2,1)S(1)}, u32[]{:S(2)}, u32[]{:S(2)}) collective-permute-start(bf16[384,512]{1,0:T(8,128)(2,1)S(1)} %copy-done.10), channel_id=1, source_target_pairs={{0,7},{1,0},{2,1},{3,2},{4,3},{5,4},{6,5},{7,6},{8,15},{9,8},{10,9... | collective-permute-start | bytes 1179656 | tf_op jit(solution)/shard_map/ppermute | solution.py:445
  23.0 7.8 %collective-permute-done.refs_4_ = bf16[384,512]{1,0:T(8,128)(2,1)S(1)} collective-permute-done((bf16[384,512]{1,0:T(8,128)(2,1)S(1)}, bf16[384,512]{1,0:T(8,128)(2,1)S(1)}, u32[]{:S(2)}, u32[]{:S(2)}) %collective-permute-start) | collective-permute-done | bytes 393248 | tf_op jit(solution)/shard_map/ppermute | solution.py:445
  34.2 4.7 %collective-permute-done.11.refs_16_ = bf16[384,512]{1,0:T(8,128)(2,1)S(1)} collective-permute-done((bf16[384,512]{1,0:T(8,128)(2,1)S(1)}, bf16[384,512]{1,0:T(8,128)(2,1)S(1)}, u32[]{:S(2)}, u32[]{:S(2)}) %collective-permute-start.11) | collective-permute-done | bytes 393248 | tf_op jit(solution)/shard_map/ppermute | solution.py:445
  38.9 3.7 %collective-permute-start.12 = (bf16[384,512]{1,0:T(8,128)(2,1)S(1)}, bf16[384,512]{1,0:T(8,128)(2,1)S(1)}, u32[]{:S(2)}, u32[]{:S(2)}) collective-permute-start(bf16[384,512]{1,0:T(8,128)(2,1)S(1)} %collective-permute-done.11.refs_16_), channel_id=1, source_target_pairs={{0,7},{1,0},{2,1},{3,2},{4,3},{5,4},{6,5},{7,6},{8,15},{9,8},{10,9... | collective-permute-start | bytes 1179656 | tf_op jit(solution)/shard_map/ppermute | solution.py:445
  42.6 5.0 %collective-permute-done.2.refs_6_ = bf16[384,512]{1,0:T(8,128)(2,1)S(1)} collective-permute-done((bf16[384,512]{1,0:T(8,128)(2,1)S(1)}, bf16[384,512]{1,0:T(8,128)(2,1)S(1)}, u32[]{:S(2)}, u32[]{:S(2)}) %collective-permute-start.2) | collective-permute-done | bytes 393248 | tf_op jit(solution)/shard_map/ppermute | solution.py:445
  51.0 4.7 %collective-permute-done.12.refs_14_ = bf16[384,512]{1,0:T(8,128)(2,1)S(1)} collective-permute-done((bf16[384,512]{1,0:T(8,128)(2,1)S(1)}, bf16[384,512]{1,0:T(8,128)(2,1)S(1)}, u32[]{:S(2)}, u32[]{:S(2)}) %collective-permute-start.12) | collective-permute-done | bytes 393248 | tf_op jit(solution)/shard_map/ppermute | solution.py:445
  55.8 3.7 %collective-permute-start.13 = (bf16[384,512]{1,0:T(8,128)(2,1)S(1)}, bf16[384,512]{1,0:T(8,128)(2,1)}, u32[]{:S(2)}, u32[]{:S(2)}) collective-permute-start(bf16[384,512]{1,0:T(8,128)(2,1)S(1)} %collective-permute-done.12.refs_14_), channel_id=1, source_target_pairs={{0,7},{1,0},{2,1},{3,2},{4,3},{5,4},{6,5},{7,6},{8,15},{9,8},{10,9... | collective-permute-start | bytes 1179656 | tf_op jit(solution)/shard_map/ppermute | solution.py:445
  59.5 5.0 %collective-permute-done.4.refs_8_ = bf16[384,512]{1,0:T(8,128)(2,1)S(1)} collective-permute-done((bf16[384,512]{1,0:T(8,128)(2,1)S(1)}, bf16[384,512]{1,0:T(8,128)(2,1)S(1)}, u32[]{:S(2)}, u32[]{:S(2)}) %collective-permute-start.4) | collective-permute-done | bytes 393248 | tf_op jit(solution)/shard_map/ppermute | solution.py:445
  68.0 4.6 %collective-permute-done.13.refs_12_ = bf16[384,512]{1,0:T(8,128)(2,1)} collective-permute-done((bf16[384,512]{1,0:T(8,128)(2,1)S(1)}, bf16[384,512]{1,0:T(8,128)(2,1)}, u32[]{:S(2)}, u32[]{:S(2)}) %collective-permute-start.13) | collective-permute-done | bytes 393248 | tf_op jit(solution)/shard_map/ppermute | solution.py:445
  73.1 8.0 %collective-permute-done.6.refs_10_ = bf16[384,512]{1,0:T(8,128)(2,1)} collective-permute-done((bf16[384,512]{1,0:T(8,128)(2,1)S(1)}, bf16[384,512]{1,0:T(8,128)(2,1)}, u32[]{:S(2)}, u32[]{:S(2)}) %collective-permute-start.6) | collective-permute-done | bytes 393248 | tf_op jit(solution)/shard_map/ppermute | solution.py:445
  81.0 9.1 %all-to-all-done = bf16[32,24,4096]{2,1,0:T(8,128)(2,1)} async-done(((bf16[32,24,4096]{2,1,0:T(8,128)(2,1)}), bf16[32,24,4096]{2,1,0:T(8,128)(2,1)}, u32[]{:S(2)}, u32[]{:S(2)}) %all-to-all-start) | async-done | bytes 6291488 | tf_op jit(solution)/shard_map/all_to_all | solution.py:492
  90.2 12.3 %terms.1 = (bf16[768,1024]{1,0:T(8,128)(2,1)}, bf16[512,768]{1,0:T(8,128)(2,1)}, bf16[2,2048,512]{2,1,0:T(8,128)(2,1)}, bf16[768,512]{1,0:T(8,128)(2,1)}, bf16[768,512]{1,0:T(8,128)(2,1)}) custom-call(s32[1]{0:T(128)} %bitcast.2.refs_0_, bf16[768,4096]{1,0:T(8,128)(2,1)} %bitcast.4.refs_1_, bf16[384,512]{1,0:T(8,128)(2,1)} %get-tuple-element.41.refs_2_, ...), custom_call_target="tpu_custom_call" | custom-call | flops 6442450944 | bytes 18874368 | tf_op jit(solution)/shard_map/terms/pallas_call | solution.py:283
  104.5 4.0 %collective-permute-start.15 = (bf16[768,512]{1,0:T(8,128)(2,1)}, bf16[768,512]{1,0:T(8,128)(2,1)}, u32[]{:S(2)}, u32[]{:S(2)}) collective-permute-start(bf16[768,512]{1,0:T(8,128)(2,1)} %get-tuple-element.49), channel_id=1, source_target_pairs={{0,7},{1,0},{2,1},{3,2},{4,3},{5,4},{6,5},{7,6},{8,15},{9,8},{10,9... | collective-permute-start | bytes 2359304 | tf_op jit(solution)/shard_map/ppermute | solution.py:445
  108.5 13.1 %rest.1 = (bf16[768,2048]{1,0:T(8,128)(2,1)}, bf16[384,512]{1,0:T(8,128)(2,1)}, bf16[384,512]{1,0:T(8,128)(2,1)}, bf16[384,512]{1,0:T(8,128)(2,1)}, bf16[384,512...) custom-call(s32[1]{0:T(128)} %bitcast.2.refs_0_, ...), custom_call_target="tpu_custom_call" | custom-call | flops 6442450944 | bytes 19922944 | tf_op jit(solution)/shard_map/rest/pallas_call | solution.py:312
  121.7 6.9 %all-to-all-start.1 = ((bf16[32,24,2048]{2,1,0:T(8,128)(2,1)}), bf16[32,24,2048]{2,1,0:T(8,128)(2,1)S(1)}, u32[]{:S(2)}, u32[]{:S(2)}) async-start(bf16[32,24,2048]{2,1,0:T(8,128)(2,1)} %bitcast.11), calls=%async_computation.1 | async-start | bytes 6291456 | tf_op jit(solution)/shard_map/all_to_all | solution.py:492
  137.1 5.2 %collective-permute-done.22 = bf16[384,512]{1,0:T(8,128)(2,1)S(1)} collective-permute-done((bf16[384,512]{1,0:T(8,128)(2,1)S(1)}, bf16[384,512]{1,0:T(8,128)(2,1)S(1)}, u32[]{:S(2)}, u32[]{:S(2)}) %collective-permute-start.22) | collective-permute-done | bytes 393248 | tf_op jit(solution)/shard_map/ppermute | solution.py:445
  142.3 4.8 %collective-permute-done.21 = bf16[384,512]{1,0:T(8,128)(2,1)S(1)} collective-permute-done((bf16[384,512]{1,0:T(8,128)(2,1)S(1)}, bf16[384,512]{1,0:T(8,128)(2,1)S(1)}, u32[]{:S(2)}, u32[]{:S(2)}) %collective-permute-start.21) | collective-permute-done | bytes 393248 | tf_op jit(solution)/shard_map/ppermute | solution.py:445
  150.7 4.8 %collective-permute-done.16 = bf16[384,512]{1,0:T(8,128)(2,1)S(1)} collective-permute-done((bf16[384,512]{1,0:T(8,128)(2,1)S(1)}, bf16[384,512]{1,0:T(8,128)(2,1)S(1)}, u32[]{:S(2)}, u32[]{:S(2)}) %collective-permute-start.16) | collective-permute-done | bytes 393248 | tf_op jit(solution)/shard_map/ppermute | solution.py:445
  159.3 4.6 %collective-permute-done.23.right_b = bf16[384,512]{1,0:T(8,128)(2,1)S(1)} collective-permute-done((bf16[384,512]{1,0:T(8,128)(2,1)S(1)}, bf16[384,512]{1,0:T(8,128)(2,1)S(1)}, u32[]{:S(2)}, u32[]{:S(2)}) %collective-permute-start.23) | collective-permute-done | bytes 393248 | tf_op jit(solution)/shard_map/ppermute | solution.py:445
  164.1 3.6 %collective-permute-done.19.left_a = bf16[384,512]{1,0:T(8,128)(2,1)S(1)} collective-permute-done((bf16[384,512]{1,0:T(8,128)(2,1)S(1)}, bf16[384,512]{1,0:T(8,128)(2,1)S(1)}, u32[]{:S(2)}, u32[]{:S(2)}) %collective-permute-start.19) | collective-permute-done | bytes 393248 | tf_op jit(solution)/shard_map/ppermute | solution.py:445
  171.4 3.9 %collective-permute-done.25.left_b = bf16[384,512]{1,0:T(8,128)(2,1)} collective-permute-done((bf16[384,512]{1,0:T(8,128)(2,1)S(1)}, bf16[384,512]{1,0:T(8,128)(2,1)}, u32[]{:S(2)}, u32[]{:S(2)}) %collective-permute-start.25) | collective-permute-done | bytes 393248 | tf_op jit(solution)/shard_map/ppermute | solution.py:445
  175.3 7.5 %collective-permute-done.20.right_a = bf16[384,512]{1,0:T(8,128)(2,1)} collective-permute-done((bf16[384,512]{1,0:T(8,128)(2,1)S(1)}, bf16[384,512]{1,0:T(8,128)(2,1)}, u32[]{:S(2)}, u32[]{:S(2)}) %collective-permute-start.20) | collective-permute-done | bytes 393248 | tf_op jit(solution)/shard_map/ppermute | solution.py:445
  (87 shorter events, 41.9 us)
Async XLA Ops:
  7.1 83.0 %all-to-all-start = ((bf16[32,24,4096]{2,1,0:T(8,128)(2,1)}), bf16[32,24,4096]{2,1,0:T(8,128)(2,1)}, u32[]{:S(2)}, u32[]{:S(2)}) async-start(bf16[32,24,4096]{2,1,0:T(8,128)(2,1)} %bitcast.10), calls=%async_computation | async-start | bytes 12582912 | tf_op jit(solution)/shard_map/all_to_all | solution.py:492
  15.0 15.9 %collective-permute-start = (bf16[384,512]{1,0:T(8,128)(2,1)S(1)}, bf16[384,512]{1,0:T(8,128)(2,1)S(1)}, u32[]{:S(2)}, u32[]{:S(2)}) collective-permute-start(bf16[384,512]{1,0:T(8,128)(2,1)S(1)} %copy-done.9), channel_id=1, source_target_pairs={{0,1},{1,2},{2,3},{3,4},{4,5},{5,6},{6,7},{7,0},{8,9},{9,10},{10,1... | collective-permute-start | bytes 1179656 | tf_op jit(solution)/shard_map/ppermute | solution.py:445
  17.0 13.9 %collective-permute-start.7 = (bf16[384,512]{1,0:T(8,128)(2,1)S(1)}, bf16[384,512]{1,0:T(8,128)(2,1)S(1)}, u32[]{:S(2)}, u32[]{:S(2)}) collective-permute-start(bf16[384,512]{1,0:T(8,128)(2,1)S(1)} %copy-done.10), channel_id=1, source_target_pairs={{0,7},{1,0},{2,1},{3,2},{4,3},{5,4},{6,5},{7,6},{8,15},{9,8},{10,9... | collective-permute-start | bytes 1179656 | tf_op jit(solution)/shard_map/ppermute | solution.py:445
  21.0 17.9 %collective-permute-start.11 = (bf16[384,512]{1,0:T(8,128)(2,1)S(1)}, bf16[384,512]{1,0:T(8,128)(2,1)S(1)}, u32[]{:S(2)}, u32[]{:S(2)}) collective-permute-start(bf16[384,512]{1,0:T(8,128)(2,1)S(1)} %copy-done.9), channel_id=1, source_target_pairs={{0,7},{1,0},{2,1},{3,2},{4,3},{5,4},{6,5},{7,6},{8,15},{9,8},{10,9... | collective-permute-start | bytes 1179656 | tf_op jit(solution)/shard_map/ppermute | solution.py:445
  23.0 19.7 %collective-permute-start.1 = (bf16[384,512]{1,0:T(8,128)(2,1)S(1)}, bf16[384,512]{1,0:T(8,128)(2,1)S(1)}, u32[]{:S(2)}, u32[]{:S(2)}) collective-permute-start(bf16[384,512]{1,0:T(8,128)(2,1)S(1)} %copy-done.10), channel_id=1, source_target_pairs={{0,1},{1,2},{2,3},{3,4},{4,5},{5,6},{6,7},{7,0},{8,9},{9,10},{10,1... | collective-permute-start | bytes 1179656 | tf_op jit(solution)/shard_map/ppermute | solution.py:445
  30.8 16.9 %collective-permute-start.2 = (bf16[384,512]{1,0:T(8,128)(2,1)S(1)}, bf16[384,512]{1,0:T(8,128)(2,1)S(1)}, u32[]{:S(2)}, u32[]{:S(2)}) collective-permute-start(bf16[384,512]{1,0:T(8,128)(2,1)S(1)} %collective-permute-done.refs_4_), channel_id=1, source_target_pairs={{0,1},{1,2},{2,3},{3,4},{4,5},{5,6},{6,7},{7,0},{8,9},{9,10},{10,1... | collective-permute-start | bytes 1179656 | tf_op jit(solution)/shard_map/ppermute | solution.py:445
  30.8 16.8 %collective-permute-start.8 = (bf16[384,512]{1,0:T(8,128)(2,1)S(1)}, bf16[384,512]{1,0:T(8,128)(2,1)S(1)}, u32[]{:S(2)}, u32[]{:S(2)}) collective-permute-start(bf16[384,512]{1,0:T(8,128)(2,1)S(1)} %collective-permute-done.7.refs_17_), channel_id=1, source_target_pairs={{0,7},{1,0},{2,1},{3,2},{4,3},{5,4},{6,5},{7,6},{8,15},{9,8},{10,9... | collective-permute-start | bytes 1179656 | tf_op jit(solution)/shard_map/ppermute | solution.py:445
  38.9 16.9 %collective-permute-start.12 = (bf16[384,512]{1,0:T(8,128)(2,1)S(1)}, bf16[384,512]{1,0:T(8,128)(2,1)S(1)}, u32[]{:S(2)}, u32[]{:S(2)}) collective-permute-start(bf16[384,512]{1,0:T(8,128)(2,1)S(1)} %collective-permute-done.11.refs_16_), channel_id=1, source_target_pairs={{0,7},{1,0},{2,1},{3,2},{4,3},{5,4},{6,5},{7,6},{8,15},{9,8},{10,9... | collective-permute-start | bytes 1179656 | tf_op jit(solution)/shard_map/ppermute | solution.py:445
  42.6 16.9 %collective-permute-start.3 = (bf16[384,512]{1,0:T(8,128)(2,1)S(1)}, bf16[384,512]{1,0:T(8,128)(2,1)S(1)}, u32[]{:S(2)}, u32[]{:S(2)}) collective-permute-start(bf16[384,512]{1,0:T(8,128)(2,1)S(1)} %collective-permute-done.1.refs_5_), channel_id=1, source_target_pairs={{0,1},{1,2},{2,3},{3,4},{4,5},{5,6},{6,7},{7,0},{8,9},{9,10},{10,1... | collective-permute-start | bytes 1179656 | tf_op jit(solution)/shard_map/ppermute | solution.py:445
  47.7 16.9 %collective-permute-start.4 = (bf16[384,512]{1,0:T(8,128)(2,1)S(1)}, bf16[384,512]{1,0:T(8,128)(2,1)S(1)}, u32[]{:S(2)}, u32[]{:S(2)}) collective-permute-start(bf16[384,512]{1,0:T(8,128)(2,1)S(1)} %collective-permute-done.2.refs_6_), channel_id=1, source_target_pairs={{0,1},{1,2},{2,3},{3,4},{4,5},{5,6},{6,7},{7,0},{8,9},{9,10},{10,1... | collective-permute-start | bytes 1179656 | tf_op jit(solution)/shard_map/ppermute | solution.py:445
  47.7 16.8 %collective-permute-start.9 = (bf16[384,512]{1,0:T(8,128)(2,1)S(1)}, bf16[384,512]{1,0:T(8,128)(2,1)}, u32[]{:S(2)}, u32[]{:S(2)}) collective-permute-start(bf16[384,512]{1,0:T(8,128)(2,1)S(1)} %collective-permute-done.8.refs_15_), channel_id=1, source_target_pairs={{0,7},{1,0},{2,1},{3,2},{4,3},{5,4},{6,5},{7,6},{8,15},{9,8},{10,9... | collective-permute-start | bytes 1179656 | tf_op jit(solution)/shard_map/ppermute | solution.py:445
  55.8 16.9 %collective-permute-start.13 = (bf16[384,512]{1,0:T(8,128)(2,1)S(1)}, bf16[384,512]{1,0:T(8,128)(2,1)}, u32[]{:S(2)}, u32[]{:S(2)}) collective-permute-start(bf16[384,512]{1,0:T(8,128)(2,1)S(1)} %collective-permute-done.12.refs_14_), channel_id=1, source_target_pairs={{0,7},{1,0},{2,1},{3,2},{4,3},{5,4},{6,5},{7,6},{8,15},{9,8},{10,9... | collective-permute-start | bytes 1179656 | tf_op jit(solution)/shard_map/ppermute | solution.py:445
  59.5 13.6 %collective-permute-start.5 = (bf16[384,512]{1,0:T(8,128)(2,1)S(1)}, bf16[384,512]{1,0:T(8,128)(2,1)}, u32[]{:S(2)}, u32[]{:S(2)}) collective-permute-start(bf16[384,512]{1,0:T(8,128)(2,1)S(1)} %collective-permute-done.3.refs_7_), channel_id=1, source_target_pairs={{0,1},{1,2},{2,3},{3,4},{4,5},{5,6},{6,7},{7,0},{8,9},{9,10},{10,1... | collective-permute-start | bytes 1179656 | tf_op jit(solution)/shard_map/ppermute | solution.py:445
  64.5 16.5 %collective-permute-start.6 = (bf16[384,512]{1,0:T(8,128)(2,1)S(1)}, bf16[384,512]{1,0:T(8,128)(2,1)}, u32[]{:S(2)}, u32[]{:S(2)}) collective-permute-start(bf16[384,512]{1,0:T(8,128)(2,1)S(1)} %collective-permute-done.4.refs_8_), channel_id=1, source_target_pairs={{0,1},{1,2},{2,3},{3,4},{4,5},{5,6},{6,7},{7,0},{8,9},{9,10},{10,1... | collective-permute-start | bytes 1179656 | tf_op jit(solution)/shard_map/ppermute | solution.py:445
  64.5 16.5 %collective-permute-start.10 = (bf16[384,512]{1,0:T(8,128)(2,1)}, bf16[384,512]{1,0:T(8,128)(2,1)}, u32[]{:S(2)}, u32[]{:S(2)}) collective-permute-start(bf16[384,512]{1,0:T(8,128)(2,1)} %collective-permute-done.9.refs_13_), channel_id=1, source_target_pairs={{0,7},{1,0},{2,1},{3,2},{4,3},{5,4},{6,5},{7,6},{8,15},{9,8},{10,9... | collective-permute-start | bytes 1179656 | tf_op jit(solution)/shard_map/ppermute | solution.py:445
  102.5 26.1 %collective-permute-start.14 = (bf16[768,512]{1,0:T(8,128)(2,1)}, bf16[768,512]{1,0:T(8,128)(2,1)}, u32[]{:S(2)}, u32[]{:S(2)}) collective-permute-start(bf16[768,512]{1,0:T(8,128)(2,1)} %get-tuple-element.48), channel_id=1, source_target_pairs={{0,1},{1,2},{2,3},{3,4},{4,5},{5,6},{6,7},{7,0},{8,9},{9,10},{10,1... | collective-permute-start | bytes 2359304 | tf_op jit(solution)/shard_map/ppermute | solution.py:445
  104.5 24.1 %collective-permute-start.15 = (bf16[768,512]{1,0:T(8,128)(2,1)}, bf16[768,512]{1,0:T(8,128)(2,1)}, u32[]{:S(2)}, u32[]{:S(2)}) collective-permute-start(bf16[768,512]{1,0:T(8,128)(2,1)} %get-tuple-element.49), channel_id=1, source_target_pairs={{0,7},{1,0},{2,1},{3,2},{4,3},{5,4},{6,5},{7,6},{8,15},{9,8},{10,9... | collective-permute-start | bytes 2359304 | tf_op jit(solution)/shard_map/ppermute | solution.py:445
  121.7 63.7 %all-to-all-start.1 = ((bf16[32,24,2048]{2,1,0:T(8,128)(2,1)}), bf16[32,24,2048]{2,1,0:T(8,128)(2,1)S(1)}, u32[]{:S(2)}, u32[]{:S(2)}) async-start(bf16[32,24,2048]{2,1,0:T(8,128)(2,1)} %bitcast.11), calls=%async_computation.1 | async-start | bytes 6291456 | tf_op jit(solution)/shard_map/all_to_all | solution.py:492
  133.8 13.3 %collective-permute-start.21 = (bf16[384,512]{1,0:T(8,128)(2,1)S(1)}, bf16[384,512]{1,0:T(8,128)(2,1)S(1)}, u32[]{:S(2)}, u32[]{:S(2)}) collective-permute-start(bf16[384,512]{1,0:T(8,128)(2,1)S(1)} %get-tuple-element.76), channel_id=1, source_target_pairs={{0,1},{1,2},{2,3},{3,4},{4,5},{5,6},{6,7},{7,0},{8,9},{9,10},{10,1... | collective-permute-start | bytes 1179656 | tf_op jit(solution)/shard_map/ppermute | solution.py:445
  134.0 16.8 %collective-permute-start.17 = (bf16[384,512]{1,0:T(8,128)(2,1)S(1)}, bf16[384,512]{1,0:T(8,128)(2,1)S(1)}, u32[]{:S(2)}, u32[]{:S(2)}) collective-permute-start(bf16[384,512]{1,0:T(8,128)(2,1)S(1)} %get-tuple-element.75), channel_id=1, source_target_pairs={{0,7},{1,0},{2,1},{3,2},{4,3},{5,4},{6,5},{7,6},{8,15},{9,8},{10,9... | collective-permute-start | bytes 1179656 | tf_op jit(solution)/shard_map/ppermute | solution.py:445
  137.1 18.4 %collective-permute-start.16 = (bf16[384,512]{1,0:T(8,128)(2,1)S(1)}, bf16[384,512]{1,0:T(8,128)(2,1)S(1)}, u32[]{:S(2)}, u32[]{:S(2)}) collective-permute-start(bf16[384,512]{1,0:T(8,128)(2,1)S(1)} %get-tuple-element.77), channel_id=1, source_target_pairs={{0,1},{1,2},{2,3},{3,4},{4,5},{5,6},{6,7},{7,0},{8,9},{9,10},{10,1... | collective-permute-start | bytes 1179656 | tf_op jit(solution)/shard_map/ppermute | solution.py:445
  147.2 12.1 %collective-permute-start.24 = (bf16[384,512]{1,0:T(8,128)(2,1)S(1)}, bf16[384,512]{1,0:T(8,128)(2,1)S(1)}, u32[]{:S(2)}, u32[]{:S(2)}) collective-permute-start(bf16[384,512]{1,0:T(8,128)(2,1)S(1)} %add_convert_fusion.1), channel_id=1, source_target_pairs={{0,7},{1,0},{2,1},{3,2},{4,3},{5,4},{6,5},{7,6},{8,15},{9,8},{10,9... | collective-permute-start | bytes 1179656 | tf_op jit(solution)/shard_map/ppermute | solution.py:445
  147.4 16.5 %collective-permute-start.23 = (bf16[384,512]{1,0:T(8,128)(2,1)S(1)}, bf16[384,512]{1,0:T(8,128)(2,1)S(1)}, u32[]{:S(2)}, u32[]{:S(2)}) collective-permute-start(bf16[384,512]{1,0:T(8,128)(2,1)S(1)} %add_convert_fusion.2), channel_id=1, source_target_pairs={{0,1},{1,2},{2,3},{3,4},{4,5},{5,6},{6,7},{7,0},{8,9},{9,10},{10,1... | collective-permute-start | bytes 1179656 | tf_op jit(solution)/shard_map/ppermute | solution.py:445
  155.8 15.4 %collective-permute-start.18 = (bf16[384,512]{1,0:T(8,128)(2,1)S(1)}, bf16[384,512]{1,0:T(8,128)(2,1)S(1)}, u32[]{:S(2)}, u32[]{:S(2)}) collective-permute-start(bf16[384,512]{1,0:T(8,128)(2,1)S(1)} %add_convert_fusion.7), channel_id=1, source_target_pairs={{0,1},{1,2},{2,3},{3,4},{4,5},{5,6},{6,7},{7,0},{8,9},{9,10},{10,1... | collective-permute-start | bytes 1179656 | tf_op jit(solution)/shard_map/ppermute | solution.py:445
  (25 other events, 690.6 us)
where the time goes:
time: 189 us; the launch traced here: 188 us
  waiting for transfers between devices  89.9 us (48%)
  starting transfers between devices  56.2 us (30%)
  Pallas kernels  34.5 us (18%)
  other arithmetic  3.73 us (2%)
  matrix products  2.76 us (1%)
    ppermute x26, waiting for transfers between devices, shift(): return lax.ppermute(a, 'dp', [(i, (i + by) % n) for i in range(n)])  80.8 us
    ppermute x26, starting transfers between devices, shift(): return lax.ppermute(a, 'dp', [(i, (i + by) % n) for i in range(n)])  41.5 us
    all_to_all x2, starting transfers between devices, exchange(): lax.all_to_all(rows.reshape(experts, capacity, rows.shape[1]), 'expert',...  14.7 us
    pallas_call x1, Pallas kernels, terms_of(): pl.pallas_call(lambda *refs: rest_kernel(parts, *refs), in_specs=[pl.Bloc...  13.1 us
    pallas_call x1, Pallas kernels, terms_of(): pl.pallas_call(lambda *refs: terms_kernel(parts, *refs), in_specs=[pl.Blo...  12.3 us
    all_to_all x2, waiting for transfers between devices, exchange(): lax.all_to_all(rows.reshape(experts, capacity, rows.shape[1]), 'expert',...  9.11 us
    pallas_call x1, Pallas kernels, pack(): pl.pallas_call(lambda *refs: pack_kernel(capacity, *refs), in_specs=[vmem...  6.47 us
  transfers between devices with their start and end apart: 28, of which 19 were waited for; matrix products, arithmetic and copies ran while one was open for 2% of the time, Pallas kernels for 8%

commit v1 on v0

--- a/solution.py
+++ b/solution.py
@@ -93,16 +93,15 @@
     steps = width // PACK_COLS
 
     def out_copy(i):
-        cols = (slice(None), pl.ds(pl.multiple_of(i * PACK_COLS, PACK_COLS), PACK_COLS))
+        cols = (slice(None), pl.ds(i * PACK_COLS, PACK_COLS))
         return pltpu.make_async_copy(packed.at[cols], packed_hbm.at[cols], out_sems.at[i])
 
     for k in range(2):
         row_copies[k].wait()
 
-        @pl.loop(0, steps)
-        def _(i):
-            source = pl.ds(pl.multiple_of(i * PACK_COLS, PACK_COLS), PACK_COLS)
-            target = pl.ds(pl.multiple_of((k * steps + i) * PACK_COLS, PACK_COLS), PACK_COLS)
+        for i in range(steps):
+            source = pl.ds(i * PACK_COLS, PACK_COLS)
+            target = pl.ds((k * steps + i) * PACK_COLS, PACK_COLS)
             packed[:, target] = matmul(place[k], tokens[k, :, source]).astype(packed.dtype)
             out_copy(k * steps + i).start()
 
@@ -513,6 +512,7 @@
     place = rank[:, None, :] == jnp.arange(capacity, dtype=jnp.int32)[None, :, None]
     place = place.reshape(experts * capacity, tok_dev).astype(jnp.bfloat16)
     token_grad = matmul(place, returned, ((0,), (0,))).astype(jnp.bfloat16)
+    token_grad, *sums = lax.optimization_barrier((token_grad, *sums))
     return (token_grad, *finish(*sums))
 
 

time: 189 us -> 186 us (0.984)
  waiting for transfers between devices: 89.9 us -> 86.7 us
    ppermute x26, waiting for transfers between devices: 80.8 us -> 77.6 us  [shift(): return lax.ppermute(a, 'dp', [(i, (i + by) % n) for i in range(n)])]
  transfers between devices with their start and end apart: 28 -> 28, of which waited for: 19 -> 19; matrix products, arithmetic and copies ran while one was open for 2% -> 4% of each run, Pallas kernels for 8% -> 7%
where the time goes in v1:
time: 186 us
  waiting for transfers between devices  86.7 us (47%)
  starting transfers between devices  56.2 us (30%)
  Pallas kernels  33.9 us (18%)
  other arithmetic  5.26 us (3%)
  matrix products  2.76 us (1%)
    ppermute x26, waiting for transfers between devices, shift(): return lax.ppermute(a, 'dp', [(i, (i + by) % n) for i in range(n)])  77.6 us
    ppermute x26, starting transfers between devices, shift(): return lax.ppermute(a, 'dp', [(i, (i + by) % n) for i in range(n)])  41.5 us
    all_to_all x2, starting transfers between devices, exchange(): lax.all_to_all(rows.reshape(experts, capacity, rows.shape[1]), 'expert',...  14.7 us
    pallas_call x1, Pallas kernels, terms_of(): pl.pallas_call(lambda *refs: rest_kernel(parts, *refs), in_specs=[pl.Bloc...  13.1 us
    pallas_call x1, Pallas kernels, terms_of(): pl.pallas_call(lambda *refs: terms_kernel(parts, *refs), in_specs=[pl.Blo...  12.3 us
    all_to_all x2, waiting for transfers between devices, exchange(): lax.all_to_all(rows.reshape(experts, capacity, rows.shape[1]), 'expert',...  9.14 us
    pallas_call x1, Pallas kernels, pack(): pl.pallas_call(lambda *refs: pack_kernel(capacity, *refs), in_specs=[vmem...  5.9 us
    convert_element_type x8, other arithmetic, ring_scatter(): arrived[c, by] = shift(total.astype(jnp.bfloat16), by)  5.26 us
  transfers between devices with their start and end apart: 28, of which 19 were waited for; matrix products, arithmetic and copies ran while one was open for 4% of the time, Pallas kernels for 7%

profile of v1, /device:TPU:2, one launch (start us, length us, event | category | flops | bytes accessed | tf_op | source)
XLA Modules:
  0.0 185.9 jit_solution(18053807884926768413)
XLA Ops:
  0.6 5.9 %pack.1 = (bf16[768,4096]{1,0:T(8,128)(2,1)}, s32[32,128]{1,0:T(8,128)}, bf16[384,512]{1,0:T(8,128)(2,1)}, bf16[384,512]{1,0:T(8,128)(2,1)}) custom-call(s32[4,128]{1,0:T(4,128)} %bitcast.12, bf16[4,128]{1,0:T(4,128)(2,1)} %bitcast.13, bf16[128,2048]{1,0:T(8,128)(2,1)} %refs_2_.1, bf16[128,2048]{1,0:T(8,128)(2,1)} %refs_3_.1, bf16[1,256,512]{2,1,0:T(8,128)(2,1)} %refs_4_.1, ...), custom_call_target="tpu_custom_call" | custom-call | flops 805306368 | bytes 6291456 | tf_op jit(solution)/shard_map/pack/pallas_call | solution.py:124
  6.6 7.8 %all-to-all-start = ((bf16[32,24,4096]{2,1,0:T(8,128)(2,1)}), bf16[32,24,4096]{2,1,0:T(8,128)(2,1)}, u32[]{:S(2)}, u32[]{:S(2)}) async-start(bf16[32,24,4096]{2,1,0:T(8,128)(2,1)} %bitcast.10), calls=%async_computation | async-start | bytes 12582912 | tf_op jit(solution)/shard_map/all_to_all | solution.py:491
  16.4 4.0 %collective-permute-start.7 = (bf16[384,512]{1,0:T(8,128)(2,1)S(1)}, bf16[384,512]{1,0:T(8,128)(2,1)S(1)}, u32[]{:S(2)}, u32[]{:S(2)}) collective-permute-start(bf16[384,512]{1,0:T(8,128)(2,1)S(1)} %copy-done.10), channel_id=1, source_target_pairs={{0,7},{1,0},{2,1},{3,2},{4,3},{5,4},{6,5},{7,6},{8,15},{9,8},{10,9... | collective-permute-start | bytes 1179656 | tf_op jit(solution)/shard_map/ppermute | solution.py:444
  22.5 7.8 %collective-permute-done.refs_4_ = bf16[384,512]{1,0:T(8,128)(2,1)S(1)} collective-permute-done((bf16[384,512]{1,0:T(8,128)(2,1)S(1)}, bf16[384,512]{1,0:T(8,128)(2,1)S(1)}, u32[]{:S(2)}, u32[]{:S(2)}) %collective-permute-start) | collective-permute-done | bytes 393248 | tf_op jit(solution)/shard_map/ppermute | solution.py:444
  33.6 4.7 %collective-permute-done.11.refs_16_ = bf16[384,512]{1,0:T(8,128)(2,1)S(1)} collective-permute-done((bf16[384,512]{1,0:T(8,128)(2,1)S(1)}, bf16[384,512]{1,0:T(8,128)(2,1)S(1)}, u32[]{:S(2)}, u32[]{:S(2)}) %collective-permute-start.11) | collective-permute-done | bytes 393248 | tf_op jit(solution)/shard_map/ppermute | solution.py:444
  38.3 3.7 %collective-permute-start.12 = (bf16[384,512]{1,0:T(8,128)(2,1)S(1)}, bf16[384,512]{1,0:T(8,128)(2,1)S(1)}, u32[]{:S(2)}, u32[]{:S(2)}) collective-permute-start(bf16[384,512]{1,0:T(8,128)(2,1)S(1)} %collective-permute-done.11.refs_16_), channel_id=1, source_target_pairs={{0,7},{1,0},{2,1},{3,2},{4,3},{5,4},{6,5},{7,6},{8,15},{9,8},{10,9... | collective-permute-start | bytes 1179656 | tf_op jit(solution)/shard_map/ppermute | solution.py:444
  42.0 5.0 %collective-permute-done.2.refs_6_ = bf16[384,512]{1,0:T(8,128)(2,1)S(1)} collective-permute-done((bf16[384,512]{1,0:T(8,128)(2,1)S(1)}, bf16[384,512]{1,0:T(8,128)(2,1)S(1)}, u32[]{:S(2)}, u32[]{:S(2)}) %collective-permute-start.2) | collective-permute-done | bytes 393248 | tf_op jit(solution)/shard_map/ppermute | solution.py:444
  50.5 4.7 %collective-permute-done.12.refs_14_ = bf16[384,512]{1,0:T(8,128)(2,1)S(1)} collective-permute-done((bf16[384,512]{1,0:T(8,128)(2,1)S(1)}, bf16[384,512]{1,0:T(8,128)(2,1)S(1)}, u32[]{:S(2)}, u32[]{:S(2)}) %collective-permute-start.12) | collective-permute-done | bytes 393248 | tf_op jit(solution)/shard_map/ppermute | solution.py:444
  55.2 3.7 %collective-permute-start.13 = (bf16[384,512]{1,0:T(8,128)(2,1)S(1)}, bf16[384,512]{1,0:T(8,128)(2,1)}, u32[]{:S(2)}, u32[]{:S(2)}) collective-permute-start(bf16[384,512]{1,0:T(8,128)(2,1)S(1)} %collective-permute-done.12.refs_14_), channel_id=1, source_target_pairs={{0,7},{1,0},{2,1},{3,2},{4,3},{5,4},{6,5},{7,6},{8,15},{9,8},{10,9... | collective-permute-start | bytes 1179656 | tf_op jit(solution)/shard_map/ppermute | solution.py:444
  58.9 5.0 %collective-permute-done.4.refs_8_ = bf16[384,512]{1,0:T(8,128)(2,1)S(1)} collective-permute-done((bf16[384,512]{1,0:T(8,128)(2,1)S(1)}, bf16[384,512]{1,0:T(8,128)(2,1)S(1)}, u32[]{:S(2)}, u32[]{:S(2)}) %collective-permute-start.4) | collective-permute-done | bytes 393248 | tf_op jit(solution)/shard_map/ppermute | solution.py:444
  63.9 3.5 %collective-permute-start.10 = (bf16[384,512]{1,0:T(8,128)(2,1)}, bf16[384,512]{1,0:T(8,128)(2,1)}, u32[]{:S(2)}, u32[]{:S(2)}) collective-permute-start(bf16[384,512]{1,0:T(8,128)(2,1)} %collective-permute-done.9.refs_13_), channel_id=1, source_target_pairs={{0,7},{1,0},{2,1},{3,2},{4,3},{5,4},{6,5},{7,6},{8,15},{9,8},{10,9... | collective-permute-start | bytes 1179656 | tf_op jit(solution)/shard_map/ppermute | solution.py:444
  67.4 4.6 %collective-permute-done.13.refs_12_ = bf16[384,512]{1,0:T(8,128)(2,1)} collective-permute-done((bf16[384,512]{1,0:T(8,128)(2,1)S(1)}, bf16[384,512]{1,0:T(8,128)(2,1)}, u32[]{:S(2)}, u32[]{:S(2)}) %collective-permute-start.13) | collective-permute-done | bytes 393248 | tf_op jit(solution)/shard_map/ppermute | solution.py:444
  72.5 8.0 %collective-permute-done.6.refs_10_ = bf16[384,512]{1,0:T(8,128)(2,1)} collective-permute-done((bf16[384,512]{1,0:T(8,128)(2,1)S(1)}, bf16[384,512]{1,0:T(8,128)(2,1)}, u32[]{:S(2)}, u32[]{:S(2)}) %collective-permute-start.6) | collective-permute-done | bytes 393248 | tf_op jit(solution)/shard_map/ppermute | solution.py:444
  80.4 9.1 %all-to-all-done = bf16[32,24,4096]{2,1,0:T(8,128)(2,1)} async-done(((bf16[32,24,4096]{2,1,0:T(8,128)(2,1)}), bf16[32,24,4096]{2,1,0:T(8,128)(2,1)}, u32[]{:S(2)}, u32[]{:S(2)}) %all-to-all-start) | async-done | bytes 6291488 | tf_op jit(solution)/shard_map/all_to_all | solution.py:491
  89.6 12.3 %terms.1 = (bf16[768,1024]{1,0:T(8,128)(2,1)}, bf16[512,768]{1,0:T(8,128)(2,1)}, bf16[2,2048,512]{2,1,0:T(8,128)(2,1)}, bf16[768,512]{1,0:T(8,128)(2,1)}, bf16[768,512]{1,0:T(8,128)(2,1)}) custom-call(s32[1]{0:T(128)} %bitcast.2.refs_0_, bf16[768,4096]{1,0:T(8,128)(2,1)} %bitcast.4.refs_1_, bf16[384,512]{1,0:T(8,128)(2,1)} %get-tuple-element.48.refs_2_, ...), custom_call_target="tpu_custom_call" | custom-call | flops 6442450944 | bytes 18874368 | tf_op jit(solution)/shard_map/terms/pallas_call | solution.py:282
  103.9 4.0 %collective-permute-start.15 = (bf16[768,512]{1,0:T(8,128)(2,1)}, bf16[768,512]{1,0:T(8,128)(2,1)}, u32[]{:S(2)}, u32[]{:S(2)}) collective-permute-start(bf16[768,512]{1,0:T(8,128)(2,1)} %get-tuple-element.56), channel_id=1, source_target_pairs={{0,7},{1,0},{2,1},{3,2},{4,3},{5,4},{6,5},{7,6},{8,15},{9,8},{10,9... | collective-permute-start | bytes 2359304 | tf_op jit(solution)/shard_map/ppermute | solution.py:444
  107.9 13.1 %rest.1 = (bf16[768,2048]{1,0:T(8,128)(2,1)}, bf16[384,512]{1,0:T(8,128)(2,1)}, bf16[384,512]{1,0:T(8,128)(2,1)}, bf16[384,512]{1,0:T(8,128)(2,1)}, bf16[384,512...) custom-call(s32[1]{0:T(128)} %bitcast.2.refs_0_, ...), custom_call_target="tpu_custom_call" | custom-call | flops 6442450944 | bytes 19922944 | tf_op jit(solution)/shard_map/rest/pallas_call | solution.py:311
  121.0 6.9 %all-to-all-start.1 = ((bf16[32,24,2048]{2,1,0:T(8,128)(2,1)}), bf16[32,24,2048]{2,1,0:T(8,128)(2,1)S(1)}, u32[]{:S(2)}, u32[]{:S(2)}) async-start(bf16[32,24,2048]{2,1,0:T(8,128)(2,1)} %bitcast.11), calls=%async_computation.1 | async-start | bytes 6291456 | tf_op jit(solution)/shard_map/all_to_all | solution.py:491
  136.7 5.0 %collective-permute-done.22 = bf16[384,512]{1,0:T(8,128)(2,1)S(1)} collective-permute-done((bf16[384,512]{1,0:T(8,128)(2,1)S(1)}, bf16[384,512]{1,0:T(8,128)(2,1)S(1)}, u32[]{:S(2)}, u32[]{:S(2)}) %collective-permute-start.22) | collective-permute-done | bytes 393248 | tf_op jit(solution)/shard_map/ppermute | solution.py:444
  141.7 5.0 %collective-permute-done.21 = bf16[384,512]{1,0:T(8,128)(2,1)S(1)} collective-permute-done((bf16[384,512]{1,0:T(8,128)(2,1)S(1)}, bf16[384,512]{1,0:T(8,128)(2,1)S(1)}, u32[]{:S(2)}, u32[]{:S(2)}) %collective-permute-start.21) | collective-permute-done | bytes 393248 | tf_op jit(solution)/shard_map/ppermute | solution.py:444
  150.1 5.0 %collective-permute-done.16 = bf16[384,512]{1,0:T(8,128)(2,1)S(1)} collective-permute-done((bf16[384,512]{1,0:T(8,128)(2,1)S(1)}, bf16[384,512]{1,0:T(8,128)(2,1)S(1)}, u32[]{:S(2)}, u32[]{:S(2)}) %collective-permute-start.16) | collective-permute-done | bytes 393248 | tf_op jit(solution)/shard_map/ppermute | solution.py:444
  158.9 4.6 %collective-permute-done.23.right_b = bf16[384,512]{1,0:T(8,128)(2,1)S(1)} collective-permute-done((bf16[384,512]{1,0:T(8,128)(2,1)S(1)}, bf16[384,512]{1,0:T(8,128)(2,1)S(1)}, u32[]{:S(2)}, u32[]{:S(2)}) %collective-permute-start.23) | collective-permute-done | bytes 393248 | tf_op jit(solution)/shard_map/ppermute | solution.py:444
  167.1 3.7 %collective-permute-done.18 = bf16[384,512]{1,0:T(8,128)(2,1)S(1)} collective-permute-done((bf16[384,512]{1,0:T(8,128)(2,1)S(1)}, bf16[384,512]{1,0:T(8,128)(2,1)S(1)}, u32[]{:S(2)}, u32[]{:S(2)}) %collective-permute-start.18) | collective-permute-done | bytes 393248 | tf_op jit(solution)/shard_map/ppermute | solution.py:444
  174.7 8.6 %collective-permute-done.20.right_a = bf16[384,512]{1,0:T(8,128)(2,1)} collective-permute-done((bf16[384,512]{1,0:T(8,128)(2,1)}, bf16[384,512]{1,0:T(8,128)(2,1)}, u32[]{:S(2)}, u32[]{:S(2)}) %collective-permute-start.20) | collective-permute-done | bytes 393248 | tf_op jit(solution)/shard_map/ppermute | solution.py:444
  (87 shorter events, 39.2 us)
Async XLA Ops:
  6.6 83.0 %all-to-all-start = ((bf16[32,24,4096]{2,1,0:T(8,128)(2,1)}), bf16[32,24,4096]{2,1,0:T(8,128)(2,1)}, u32[]{:S(2)}, u32[]{:S(2)}) async-start(bf16[32,24,4096]{2,1,0:T(8,128)(2,1)} %bitcast.10), calls=%async_computation | async-start | bytes 12582912 | tf_op jit(solution)/shard_map/all_to_all | solution.py:491
  14.4 15.8 %collective-permute-start = (bf16[384,512]{1,0:T(8,128)(2,1)S(1)}, bf16[384,512]{1,0:T(8,128)(2,1)S(1)}, u32[]{:S(2)}, u32[]{:S(2)}) collective-permute-start(bf16[384,512]{1,0:T(8,128)(2,1)S(1)} %copy-done.9), channel_id=1, source_target_pairs={{0,1},{1,2},{2,3},{3,4},{4,5},{5,6},{6,7},{7,0},{8,9},{9,10},{10,1... | collective-permute-start | bytes 1179656 | tf_op jit(solution)/shard_map/ppermute | solution.py:444
  16.4 13.8 %collective-permute-start.7 = (bf16[384,512]{1,0:T(8,128)(2,1)S(1)}, bf16[384,512]{1,0:T(8,128)(2,1)S(1)}, u32[]{:S(2)}, u32[]{:S(2)}) collective-permute-start(bf16[384,512]{1,0:T(8,128)(2,1)S(1)} %copy-done.10), channel_id=1, source_target_pairs={{0,7},{1,0},{2,1},{3,2},{4,3},{5,4},{6,5},{7,6},{8,15},{9,8},{10,9... | collective-permute-start | bytes 1179656 | tf_op jit(solution)/shard_map/ppermute | solution.py:444
  20.4 17.9 %collective-permute-start.11 = (bf16[384,512]{1,0:T(8,128)(2,1)S(1)}, bf16[384,512]{1,0:T(8,128)(2,1)S(1)}, u32[]{:S(2)}, u32[]{:S(2)}) collective-permute-start(bf16[384,512]{1,0:T(8,128)(2,1)S(1)} %copy-done.9), channel_id=1, source_target_pairs={{0,7},{1,0},{2,1},{3,2},{4,3},{5,4},{6,5},{7,6},{8,15},{9,8},{10,9... | collective-permute-start | bytes 1179656 | tf_op jit(solution)/shard_map/ppermute | solution.py:444
  22.4 19.7 %collective-permute-start.1 = (bf16[384,512]{1,0:T(8,128)(2,1)S(1)}, bf16[384,512]{1,0:T(8,128)(2,1)S(1)}, u32[]{:S(2)}, u32[]{:S(2)}) collective-permute-start(bf16[384,512]{1,0:T(8,128)(2,1)S(1)} %copy-done.10), channel_id=1, source_target_pairs={{0,1},{1,2},{2,3},{3,4},{4,5},{5,6},{6,7},{7,0},{8,9},{9,10},{10,1... | collective-permute-start | bytes 1179656 | tf_op jit(solution)/shard_map/ppermute | solution.py:444
  30.2 16.9 %collective-permute-start.2 = (bf16[384,512]{1,0:T(8,128)(2,1)S(1)}, bf16[384,512]{1,0:T(8,128)(2,1)S(1)}, u32[]{:S(2)}, u32[]{:S(2)}) collective-permute-start(bf16[384,512]{1,0:T(8,128)(2,1)S(1)} %collective-permute-done.refs_4_), channel_id=1, source_target_pairs={{0,1},{1,2},{2,3},{3,4},{4,5},{5,6},{6,7},{7,0},{8,9},{9,10},{10,1... | collective-permute-start | bytes 1179656 | tf_op jit(solution)/shard_map/ppermute | solution.py:444
  30.2 16.8 %collective-permute-start.8 = (bf16[384,512]{1,0:T(8,128)(2,1)S(1)}, bf16[384,512]{1,0:T(8,128)(2,1)S(1)}, u32[]{:S(2)}, u32[]{:S(2)}) collective-permute-start(bf16[384,512]{1,0:T(8,128)(2,1)S(1)} %collective-permute-done.7.refs_17_), channel_id=1, source_target_pairs={{0,7},{1,0},{2,1},{3,2},{4,3},{5,4},{6,5},{7,6},{8,15},{9,8},{10,9... | collective-permute-start | bytes 1179656 | tf_op jit(solution)/shard_map/ppermute | solution.py:444
  38.3 16.9 %collective-permute-start.12 = (bf16[384,512]{1,0:T(8,128)(2,1)S(1)}, bf16[384,512]{1,0:T(8,128)(2,1)S(1)}, u32[]{:S(2)}, u32[]{:S(2)}) collective-permute-start(bf16[384,512]{1,0:T(8,128)(2,1)S(1)} %collective-permute-done.11.refs_16_), channel_id=1, source_target_pairs={{0,7},{1,0},{2,1},{3,2},{4,3},{5,4},{6,5},{7,6},{8,15},{9,8},{10,9... | collective-permute-start | bytes 1179656 | tf_op jit(solution)/shard_map/ppermute | solution.py:444
  42.0 16.9 %collective-permute-start.3 = (bf16[384,512]{1,0:T(8,128)(2,1)S(1)}, bf16[384,512]{1,0:T(8,128)(2,1)S(1)}, u32[]{:S(2)}, u32[]{:S(2)}) collective-permute-start(bf16[384,512]{1,0:T(8,128)(2,1)S(1)} %collective-permute-done.1.refs_5_), channel_id=1, source_target_pairs={{0,1},{1,2},{2,3},{3,4},{4,5},{5,6},{6,7},{7,0},{8,9},{9,10},{10,1... | collective-permute-start | bytes 1179656 | tf_op jit(solution)/shard_map/ppermute | solution.py:444
  47.1 16.9 %collective-permute-start.4 = (bf16[384,512]{1,0:T(8,128)(2,1)S(1)}, bf16[384,512]{1,0:T(8,128)(2,1)S(1)}, u32[]{:S(2)}, u32[]{:S(2)}) collective-permute-start(bf16[384,512]{1,0:T(8,128)(2,1)S(1)} %collective-permute-done.2.refs_6_), channel_id=1, source_target_pairs={{0,1},{1,2},{2,3},{3,4},{4,5},{5,6},{6,7},{7,0},{8,9},{9,10},{10,1... | collective-permute-start | bytes 1179656 | tf_op jit(solution)/shard_map/ppermute | solution.py:444
  47.1 16.8 %collective-permute-start.9 = (bf16[384,512]{1,0:T(8,128)(2,1)S(1)}, bf16[384,512]{1,0:T(8,128)(2,1)}, u32[]{:S(2)}, u32[]{:S(2)}) collective-permute-start(bf16[384,512]{1,0:T(8,128)(2,1)S(1)} %collective-permute-done.8.refs_15_), channel_id=1, source_target_pairs={{0,7},{1,0},{2,1},{3,2},{4,3},{5,4},{6,5},{7,6},{8,15},{9,8},{10,9... | collective-permute-start | bytes 1179656 | tf_op jit(solution)/shard_map/ppermute | solution.py:444
  55.2 16.9 %collective-permute-start.13 = (bf16[384,512]{1,0:T(8,128)(2,1)S(1)}, bf16[384,512]{1,0:T(8,128)(2,1)}, u32[]{:S(2)}, u32[]{:S(2)}) collective-permute-start(bf16[384,512]{1,0:T(8,128)(2,1)S(1)} %collective-permute-done.12.refs_14_), channel_id=1, source_target_pairs={{0,7},{1,0},{2,1},{3,2},{4,3},{5,4},{6,5},{7,6},{8,15},{9,8},{10,9... | collective-permute-start | bytes 1179656 | tf_op jit(solution)/shard_map/ppermute | solution.py:444
  58.9 13.6 %collective-permute-start.5 = (bf16[384,512]{1,0:T(8,128)(2,1)S(1)}, bf16[384,512]{1,0:T(8,128)(2,1)}, u32[]{:S(2)}, u32[]{:S(2)}) collective-permute-start(bf16[384,512]{1,0:T(8,128)(2,1)S(1)} %collective-permute-done.3.refs_7_), channel_id=1, source_target_pairs={{0,1},{1,2},{2,3},{3,4},{4,5},{5,6},{6,7},{7,0},{8,9},{9,10},{10,1... | collective-permute-start | bytes 1179656 | tf_op jit(solution)/shard_map/ppermute | solution.py:444
  63.9 16.5 %collective-permute-start.6 = (bf16[384,512]{1,0:T(8,128)(2,1)S(1)}, bf16[384,512]{1,0:T(8,128)(2,1)}, u32[]{:S(2)}, u32[]{:S(2)}) collective-permute-start(bf16[384,512]{1,0:T(8,128)(2,1)S(1)} %collective-permute-done.4.refs_8_), channel_id=1, source_target_pairs={{0,1},{1,2},{2,3},{3,4},{4,5},{5,6},{6,7},{7,0},{8,9},{9,10},{10,1... | collective-permute-start | bytes 1179656 | tf_op jit(solution)/shard_map/ppermute | solution.py:444
  63.9 16.5 %collective-permute-start.10 = (bf16[384,512]{1,0:T(8,128)(2,1)}, bf16[384,512]{1,0:T(8,128)(2,1)}, u32[]{:S(2)}, u32[]{:S(2)}) collective-permute-start(bf16[384,512]{1,0:T(8,128)(2,1)} %collective-permute-done.9.refs_13_), channel_id=1, source_target_pairs={{0,7},{1,0},{2,1},{3,2},{4,3},{5,4},{6,5},{7,6},{8,15},{9,8},{10,9... | collective-permute-start | bytes 1179656 | tf_op jit(solution)/shard_map/ppermute | solution.py:444
  101.9 26.0 %collective-permute-start.14 = (bf16[768,512]{1,0:T(8,128)(2,1)}, bf16[768,512]{1,0:T(8,128)(2,1)}, u32[]{:S(2)}, u32[]{:S(2)}) collective-permute-start(bf16[768,512]{1,0:T(8,128)(2,1)} %get-tuple-element.55), channel_id=1, source_target_pairs={{0,1},{1,2},{2,3},{3,4},{4,5},{5,6},{6,7},{7,0},{8,9},{9,10},{10,1... | collective-permute-start | bytes 2359304 | tf_op jit(solution)/shard_map/ppermute | solution.py:444
  103.9 24.0 %collective-permute-start.15 = (bf16[768,512]{1,0:T(8,128)(2,1)}, bf16[768,512]{1,0:T(8,128)(2,1)}, u32[]{:S(2)}, u32[]{:S(2)}) collective-permute-start(bf16[768,512]{1,0:T(8,128)(2,1)} %get-tuple-element.56), channel_id=1, source_target_pairs={{0,7},{1,0},{2,1},{3,2},{4,3},{5,4},{6,5},{7,6},{8,15},{9,8},{10,9... | collective-permute-start | bytes 2359304 | tf_op jit(solution)/shard_map/ppermute | solution.py:444
  121.0 50.7 %all-to-all-start.1 = ((bf16[32,24,2048]{2,1,0:T(8,128)(2,1)}), bf16[32,24,2048]{2,1,0:T(8,128)(2,1)S(1)}, u32[]{:S(2)}, u32[]{:S(2)}) async-start(bf16[32,24,2048]{2,1,0:T(8,128)(2,1)} %bitcast.11), calls=%async_computation.1 | async-start | bytes 6291456 | tf_op jit(solution)/shard_map/all_to_all | solution.py:491
  133.2 13.5 %collective-permute-start.21 = (bf16[384,512]{1,0:T(8,128)(2,1)S(1)}, bf16[384,512]{1,0:T(8,128)(2,1)S(1)}, u32[]{:S(2)}, u32[]{:S(2)}) collective-permute-start(bf16[384,512]{1,0:T(8,128)(2,1)S(1)} %get-tuple-element.90), channel_id=1, source_target_pairs={{0,1},{1,2},{2,3},{3,4},{4,5},{5,6},{6,7},{7,0},{8,9},{9,10},{10,1... | collective-permute-start | bytes 1179656 | tf_op jit(solution)/shard_map/ppermute | solution.py:444
  133.5 16.5 %collective-permute-start.17 = (bf16[384,512]{1,0:T(8,128)(2,1)S(1)}, bf16[384,512]{1,0:T(8,128)(2,1)S(1)}, u32[]{:S(2)}, u32[]{:S(2)}) collective-permute-start(bf16[384,512]{1,0:T(8,128)(2,1)S(1)} %get-tuple-element.89), channel_id=1, source_target_pairs={{0,7},{1,0},{2,1},{3,2},{4,3},{5,4},{6,5},{7,6},{8,15},{9,8},{10,9... | collective-permute-start | bytes 1179656 | tf_op jit(solution)/shard_map/ppermute | solution.py:444
  136.7 18.4 %collective-permute-start.16 = (bf16[384,512]{1,0:T(8,128)(2,1)S(1)}, bf16[384,512]{1,0:T(8,128)(2,1)S(1)}, u32[]{:S(2)}, u32[]{:S(2)}) collective-permute-start(bf16[384,512]{1,0:T(8,128)(2,1)S(1)} %get-tuple-element.91), channel_id=1, source_target_pairs={{0,1},{1,2},{2,3},{3,4},{4,5},{5,6},{6,7},{7,0},{8,9},{9,10},{10,1... | collective-permute-start | bytes 1179656 | tf_op jit(solution)/shard_map/ppermute | solution.py:444
  146.8 12.1 %collective-permute-start.24 = (bf16[384,512]{1,0:T(8,128)(2,1)S(1)}, bf16[384,512]{1,0:T(8,128)(2,1)S(1)}, u32[]{:S(2)}, u32[]{:S(2)}) collective-permute-start(bf16[384,512]{1,0:T(8,128)(2,1)S(1)} %add_convert_fusion.1), channel_id=1, source_target_pairs={{0,7},{1,0},{2,1},{3,2},{4,3},{5,4},{6,5},{7,6},{8,15},{9,8},{10,9... | collective-permute-start | bytes 1179656 | tf_op jit(solution)/shard_map/ppermute | solution.py:444
  147.0 16.5 %collective-permute-start.23 = (bf16[384,512]{1,0:T(8,128)(2,1)S(1)}, bf16[384,512]{1,0:T(8,128)(2,1)S(1)}, u32[]{:S(2)}, u32[]{:S(2)}) collective-permute-start(bf16[384,512]{1,0:T(8,128)(2,1)S(1)} %add_convert_fusion.2), channel_id=1, source_target_pairs={{0,1},{1,2},{2,3},{3,4},{4,5},{5,6},{6,7},{7,0},{8,9},{9,10},{10,1... | collective-permute-start | bytes 1179656 | tf_op jit(solution)/shard_map/ppermute | solution.py:444
  155.4 15.4 %collective-permute-start.18 = (bf16[384,512]{1,0:T(8,128)(2,1)S(1)}, bf16[384,512]{1,0:T(8,128)(2,1)S(1)}, u32[]{:S(2)}, u32[]{:S(2)}) collective-permute-start(bf16[384,512]{1,0:T(8,128)(2,1)S(1)} %add_convert_fusion.7), channel_id=1, source_target_pairs={{0,1},{1,2},{2,3},{3,4},{4,5},{5,6},{6,7},{7,0},{8,9},{9,10},{10,1... | collective-permute-start | bytes 1179656 | tf_op jit(solution)/shard_map/ppermute | solution.py:444
  (25 other events, 668.0 us)

commit v2 on v1

--- a/solution.py
+++ b/solution.py
@@ -467,17 +467,16 @@
         for c in range(2)
     }
     for _ in range(n // 2):
-        for c in range(2):
-            going = [by for by in (1, -1) if left[c, by] > 1]
-            for by in going:
+        for group in (((0, 1), (1, -1)), ((1, 1), (0, -1))):
+            going = [key for key in group if left[key] > 1]
+            for c, by in going:
                 left[c, by] -= 1
                 mine = own[by * left[c, by] % n, c].astype(jnp.float32)
                 total = arrived[c, by].astype(jnp.float32) + mine
                 arrived[c, by] = shift(total.astype(jnp.bfloat16), by)
-            if len(going) == 2:
-                arrived[c, 1], arrived[c, -1] = lax.optimization_barrier(
-                    (arrived[c, 1], arrived[c, -1])
-                )
+            if any(left[key] > 1 for key in going):
+                met = lax.optimization_barrier([arrived[key] for key in going])
+                arrived.update(zip(going, met))
     return [a for c in range(2) for a in (own[0, c], arrived[c, 1], arrived[c, -1])]
 
 

time: 186 us -> 186 us (level)
  waiting for transfers between devices: 86.7 us -> 81.5 us
  starting transfers between devices: 56.2 us -> 59.3 us
    ppermute x26, waiting for transfers between devices: 77.6 us -> 72.4 us  [shift(): return lax.ppermute(a, 'dp', [(i, (i + by) % n) for i in range(n)])]
    ppermute x26, starting transfers between devices: 41.5 us -> 44.6 us  [shift(): return lax.ppermute(a, 'dp', [(i, (i + by) % n) for i in range(n)])]
  transfers between devices with their start and end apart: 28 -> 28, of which waited for: 19 -> 18; matrix products, arithmetic and copies ran while one was open for 4% -> 5% of each run, Pallas kernels for 7% -> 7%
where the time goes in v2:
time: 186 us; the launch traced here: 185 us
  waiting for transfers between devices  81.5 us (44%)
  starting transfers between devices  59.3 us (32%)
  Pallas kernels  33.8 us (18%)
  other arithmetic  6.76 us (4%)
  matrix products  2.76 us (1%)
    ppermute x26, waiting for transfers between devices, shift(): return lax.ppermute(a, 'dp', [(i, (i + by) % n) for i in range(n)])  72.4 us
    ppermute x26, starting transfers between devices, shift(): return lax.ppermute(a, 'dp', [(i, (i + by) % n) for i in range(n)])  44.6 us
    all_to_all x2, starting transfers between devices, exchange(): lax.all_to_all(rows.reshape(experts, capacity, rows.shape[1]), 'expert',...  14.7 us
    pallas_call x1, Pallas kernels, terms_of(): pl.pallas_call(lambda *refs: rest_kernel(parts, *refs), in_specs=[pl.Bloc...  13.1 us
    pallas_call x1, Pallas kernels, terms_of(): pl.pallas_call(lambda *refs: terms_kernel(parts, *refs), in_specs=[pl.Blo...  12.3 us
    all_to_all x2, waiting for transfers between devices, exchange(): lax.all_to_all(rows.reshape(experts, capacity, rows.shape[1]), 'expert',...  9.14 us
    convert_element_type x8, other arithmetic, ring_scatter(): arrived[c, by] = shift(total.astype(jnp.bfloat16), by)  6.76 us
    pallas_call x1, Pallas kernels, pack(): pl.pallas_call(lambda *refs: pack_kernel(capacity, *refs), in_specs=[vmem...  5.88 us
  transfers between devices with their start and end apart: 28, of which 18 were waited for; matrix products, arithmetic and copies ran while one was open for 5% of the time, Pallas kernels for 7%

profile of v2, /device:TPU:2, one launch (start us, length us, event | category | flops | bytes accessed | tf_op | source)
XLA Modules:
  0.0 185.2 jit_solution(4471096470921746200)
XLA Ops:
  0.6 5.9 %pack.1 = (bf16[768,4096]{1,0:T(8,128)(2,1)}, s32[32,128]{1,0:T(8,128)}, bf16[384,512]{1,0:T(8,128)(2,1)}, bf16[384,512]{1,0:T(8,128)(2,1)}) custom-call(s32[4,128]{1,0:T(4,128)} %bitcast.12, bf16[4,128]{1,0:T(4,128)(2,1)} %bitcast.13, bf16[128,2048]{1,0:T(8,128)(2,1)} %refs_2_.1, bf16[128,2048]{1,0:T(8,128)(2,1)} %refs_3_.1, bf16[1,256,512]{2,1,0:T(8,128)(2,1)} %refs_4_.1, ...), custom_call_target="tpu_custom_call" | custom-call | flops 805306368 | bytes 6291456 | tf_op jit(solution)/shard_map/pack/pallas_call | solution.py:124
  6.5 7.8 %all-to-all-start = ((bf16[32,24,4096]{2,1,0:T(8,128)(2,1)}), bf16[32,24,4096]{2,1,0:T(8,128)(2,1)}, u32[]{:S(2)}, u32[]{:S(2)}) async-start(bf16[32,24,4096]{2,1,0:T(8,128)(2,1)} %bitcast.10), calls=%async_computation | async-start | bytes 12582912 | tf_op jit(solution)/shard_map/all_to_all | solution.py:490
  16.4 4.0 %collective-permute-start.7 = (bf16[384,512]{1,0:T(8,128)(2,1)S(1)}, bf16[384,512]{1,0:T(8,128)(2,1)S(1)}, u32[]{:S(2)}, u32[]{:S(2)}) collective-permute-start(bf16[384,512]{1,0:T(8,128)(2,1)S(1)} %copy-done.9), channel_id=1, source_target_pairs={{0,7},{1,0},{2,1},{3,2},{4,3},{5,4},{6,5},{7,6},{8,15},{9,8},{10,9... | collective-permute-start | bytes 1179656 | tf_op jit(solution)/shard_map/ppermute | solution.py:444
  22.4 7.8 %collective-permute-done.refs_4_ = bf16[384,512]{1,0:T(8,128)(2,1)S(1)} collective-permute-done((bf16[384,512]{1,0:T(8,128)(2,1)S(1)}, bf16[384,512]{1,0:T(8,128)(2,1)S(1)}, u32[]{:S(2)}, u32[]{:S(2)}) %collective-permute-start) | collective-permute-done | bytes 393248 | tf_op jit(solution)/shard_map/ppermute | solution.py:444
  30.2 3.4 %collective-permute-start.8 = (bf16[384,512]{1,0:T(8,128)(2,1)S(1)}, bf16[384,512]{1,0:T(8,128)(2,1)S(1)}, u32[]{:S(2)}, u32[]{:S(2)}) collective-permute-start(bf16[384,512]{1,0:T(8,128)(2,1)S(1)} %collective-permute-done.7.refs_17_), channel_id=1, source_target_pairs={{0,7},{1,0},{2,1},{3,2},{4,3},{5,4},{6,5},{7,6},{8,15},{9,8},{10,9... | collective-permute-start | bytes 1179656 | tf_op jit(solution)/shard_map/ppermute | solution.py:444
  33.6 4.7 %collective-permute-done.11.refs_16_ = bf16[384,512]{1,0:T(8,128)(2,1)S(1)} collective-permute-done((bf16[384,512]{1,0:T(8,128)(2,1)S(1)}, bf16[384,512]{1,0:T(8,128)(2,1)S(1)}, u32[]{:S(2)}, u32[]{:S(2)}) %collective-permute-start.11) | collective-permute-done | bytes 393248 | tf_op jit(solution)/shard_map/ppermute | solution.py:444
  38.3 3.7 %collective-permute-start.12 = (bf16[384,512]{1,0:T(8,128)(2,1)S(1)}, bf16[384,512]{1,0:T(8,128)(2,1)S(1)}, u32[]{:S(2)}, u32[]{:S(2)}) collective-permute-start(bf16[384,512]{1,0:T(8,128)(2,1)S(1)} %collective-permute-done.11.refs_16_), channel_id=1, source_target_pairs={{0,7},{1,0},{2,1},{3,2},{4,3},{5,4},{6,5},{7,6},{8,15},{9,8},{10,9... | collective-permute-start | bytes 1179656 | tf_op jit(solution)/shard_map/ppermute | solution.py:444
  42.0 5.0 %collective-permute-done.2.refs_6_ = bf16[384,512]{1,0:T(8,128)(2,1)S(1)} collective-permute-done((bf16[384,512]{1,0:T(8,128)(2,1)S(1)}, bf16[384,512]{1,0:T(8,128)(2,1)S(1)}, u32[]{:S(2)}, u32[]{:S(2)}) %collective-permute-start.2) | collective-permute-done | bytes 393248 | tf_op jit(solution)/shard_map/ppermute | solution.py:444
  50.4 4.7 %collective-permute-done.12.refs_14_ = bf16[384,512]{1,0:T(8,128)(2,1)S(1)} collective-permute-done((bf16[384,512]{1,0:T(8,128)(2,1)S(1)}, bf16[384,512]{1,0:T(8,128)(2,1)S(1)}, u32[]{:S(2)}, u32[]{:S(2)}) %collective-permute-start.12) | collective-permute-done | bytes 393248 | tf_op jit(solution)/shard_map/ppermute | solution.py:444
  55.2 3.7 %collective-permute-start.13 = (bf16[384,512]{1,0:T(8,128)(2,1)S(1)}, bf16[384,512]{1,0:T(8,128)(2,1)}, u32[]{:S(2)}, u32[]{:S(2)}) collective-permute-start(bf16[384,512]{1,0:T(8,128)(2,1)S(1)} %collective-permute-done.12.refs_14_), channel_id=1, source_target_pairs={{0,7},{1,0},{2,1},{3,2},{4,3},{5,4},{6,5},{7,6},{8,15},{9,8},{10,9... | collective-permute-start | bytes 1179656 | tf_op jit(solution)/shard_map/ppermute | solution.py:444
  58.9 5.0 %collective-permute-done.4.refs_8_ = bf16[384,512]{1,0:T(8,128)(2,1)S(1)} collective-permute-done((bf16[384,512]{1,0:T(8,128)(2,1)S(1)}, bf16[384,512]{1,0:T(8,128)(2,1)S(1)}, u32[]{:S(2)}, u32[]{:S(2)}) %collective-permute-start.4) | collective-permute-done | bytes 393248 | tf_op jit(solution)/shard_map/ppermute | solution.py:444
  63.9 3.5 %collective-permute-start.10 = (bf16[384,512]{1,0:T(8,128)(2,1)}, bf16[384,512]{1,0:T(8,128)(2,1)}, u32[]{:S(2)}, u32[]{:S(2)}) collective-permute-start(bf16[384,512]{1,0:T(8,128)(2,1)} %collective-permute-done.9.refs_13_), channel_id=1, source_target_pairs={{0,7},{1,0},{2,1},{3,2},{4,3},{5,4},{6,5},{7,6},{8,15},{9,8},{10,9... | collective-permute-start | bytes 1179656 | tf_op jit(solution)/shard_map/ppermute | solution.py:444
  67.4 4.6 %collective-permute-done.13.refs_12_ = bf16[384,512]{1,0:T(8,128)(2,1)} collective-permute-done((bf16[384,512]{1,0:T(8,128)(2,1)S(1)}, bf16[384,512]{1,0:T(8,128)(2,1)}, u32[]{:S(2)}, u32[]{:S(2)}) %collective-permute-start.13) | collective-permute-done | bytes 393248 | tf_op jit(solution)/shard_map/ppermute | solution.py:444
  72.4 8.0 %collective-permute-done.6.refs_10_ = bf16[384,512]{1,0:T(8,128)(2,1)} collective-permute-done((bf16[384,512]{1,0:T(8,128)(2,1)S(1)}, bf16[384,512]{1,0:T(8,128)(2,1)}, u32[]{:S(2)}, u32[]{:S(2)}) %collective-permute-start.6) | collective-permute-done | bytes 393248 | tf_op jit(solution)/shard_map/ppermute | solution.py:444
  80.4 9.1 %all-to-all-done = bf16[32,24,4096]{2,1,0:T(8,128)(2,1)} async-done(((bf16[32,24,4096]{2,1,0:T(8,128)(2,1)}), bf16[32,24,4096]{2,1,0:T(8,128)(2,1)}, u32[]{:S(2)}, u32[]{:S(2)}) %all-to-all-start) | async-done | bytes 6291488 | tf_op jit(solution)/shard_map/all_to_all | solution.py:490
  89.6 12.3 %terms.1 = (bf16[768,1024]{1,0:T(8,128)(2,1)}, bf16[512,768]{1,0:T(8,128)(2,1)}, bf16[2,2048,512]{2,1,0:T(8,128)(2,1)}, bf16[768,512]{1,0:T(8,128)(2,1)}, bf16[768,512]{1,0:T(8,128)(2,1)}) custom-call(s32[1]{0:T(128)} %bitcast.2.refs_0_, bf16[768,4096]{1,0:T(8,128)(2,1)} %bitcast.4.refs_1_, bf16[384,512]{1,0:T(8,128)(2,1)} %get-tuple-element.46.refs_2_, ...), custom_call_target="tpu_custom_call" | custom-call | flops 6442450944 | bytes 18874368 | tf_op jit(solution)/shard_map/terms/pallas_call | solution.py:282
  103.9 4.0 %collective-permute-start.15 = (bf16[768,512]{1,0:T(8,128)(2,1)}, bf16[768,512]{1,0:T(8,128)(2,1)}, u32[]{:S(2)}, u32[]{:S(2)}) collective-permute-start(bf16[768,512]{1,0:T(8,128)(2,1)} %get-tuple-element.54), channel_id=1, source_target_pairs={{0,7},{1,0},{2,1},{3,2},{4,3},{5,4},{6,5},{7,6},{8,15},{9,8},{10,9... | collective-permute-start | bytes 2359304 | tf_op jit(solution)/shard_map/ppermute | solution.py:444
  107.9 13.1 %rest.1 = (bf16[768,2048]{1,0:T(8,128)(2,1)}, bf16[384,512]{1,0:T(8,128)(2,1)}, bf16[384,512]{1,0:T(8,128)(2,1)}, bf16[384,512]{1,0:T(8,128)(2,1)}, bf16[384,512...) custom-call(s32[1]{0:T(128)} %bitcast.2.refs_0_, ...), custom_call_target="tpu_custom_call" | custom-call | flops 6442450944 | bytes 19922944 | tf_op jit(solution)/shard_map/rest/pallas_call | solution.py:311
  121.0 6.9 %all-to-all-start.1 = ((bf16[32,24,2048]{2,1,0:T(8,128)(2,1)}), bf16[32,24,2048]{2,1,0:T(8,128)(2,1)S(1)}, u32[]{:S(2)}, u32[]{:S(2)}) async-start(bf16[32,24,2048]{2,1,0:T(8,128)(2,1)} %bitcast.11), calls=%async_computation.1 | async-start | bytes 6291456 | tf_op jit(solution)/shard_map/all_to_all | solution.py:490
  136.7 4.9 %collective-permute-done.22 = bf16[384,512]{1,0:T(8,128)(2,1)S(1)} collective-permute-done((bf16[384,512]{1,0:T(8,128)(2,1)S(1)}, bf16[384,512]{1,0:T(8,128)(2,1)S(1)}, u32[]{:S(2)}, u32[]{:S(2)}) %collective-permute-start.22) | collective-permute-done | bytes 393248 | tf_op jit(solution)/shard_map/ppermute | solution.py:444
  141.6 5.0 %collective-permute-done.21 = bf16[384,512]{1,0:T(8,128)(2,1)S(1)} collective-permute-done((bf16[384,512]{1,0:T(8,128)(2,1)S(1)}, bf16[384,512]{1,0:T(8,128)(2,1)S(1)}, u32[]{:S(2)}, u32[]{:S(2)}) %collective-permute-start.21) | collective-permute-done | bytes 393248 | tf_op jit(solution)/shard_map/ppermute | solution.py:444
  149.3 4.7 %collective-permute-done.16 = bf16[384,512]{1,0:T(8,128)(2,1)S(1)} collective-permute-done((bf16[384,512]{1,0:T(8,128)(2,1)S(1)}, bf16[384,512]{1,0:T(8,128)(2,1)S(1)}, u32[]{:S(2)}, u32[]{:S(2)}) %collective-permute-start.16) | collective-permute-done | bytes 393248 | tf_op jit(solution)/shard_map/ppermute | solution.py:444
  161.3 4.9 %collective-permute-done.19 = bf16[384,512]{1,0:T(8,128)(2,1)S(1)} collective-permute-done((bf16[384,512]{1,0:T(8,128)(2,1)S(1)}, bf16[384,512]{1,0:T(8,128)(2,1)S(1)}, u32[]{:S(2)}, u32[]{:S(2)}) %collective-permute-start.19) | collective-permute-done | bytes 393248 | tf_op jit(solution)/shard_map/ppermute | solution.py:444
  176.1 5.1 %collective-permute-done.25.left_b = bf16[384,512]{1,0:T(8,128)(2,1)} collective-permute-done((bf16[384,512]{1,0:T(8,128)(2,1)}, bf16[384,512]{1,0:T(8,128)(2,1)}, u32[]{:S(2)}, u32[]{:S(2)}) %collective-permute-start.25) | collective-permute-done | bytes 393248 | tf_op jit(solution)/shard_map/ppermute | solution.py:444
  (85 shorter events, 42.4 us)
Async XLA Ops:
  6.5 83.0 %all-to-all-start = ((bf16[32,24,4096]{2,1,0:T(8,128)(2,1)}), bf16[32,24,4096]{2,1,0:T(8,128)(2,1)}, u32[]{:S(2)}, u32[]{:S(2)}) async-start(bf16[32,24,4096]{2,1,0:T(8,128)(2,1)} %bitcast.10), calls=%async_computation | async-start | bytes 12582912 | tf_op jit(solution)/shard_map/all_to_all | solution.py:490
  14.4 15.8 %collective-permute-start = (bf16[384,512]{1,0:T(8,128)(2,1)S(1)}, bf16[384,512]{1,0:T(8,128)(2,1)S(1)}, u32[]{:S(2)}, u32[]{:S(2)}) collective-permute-start(bf16[384,512]{1,0:T(8,128)(2,1)S(1)} %copy-done.8), channel_id=1, source_target_pairs={{0,1},{1,2},{2,3},{3,4},{4,5},{5,6},{6,7},{7,0},{8,9},{9,10},{10,1... | collective-permute-start | bytes 1179656 | tf_op jit(solution)/shard_map/ppermute | solution.py:444
  16.4 13.8 %collective-permute-start.7 = (bf16[384,512]{1,0:T(8,128)(2,1)S(1)}, bf16[384,512]{1,0:T(8,128)(2,1)S(1)}, u32[]{:S(2)}, u32[]{:S(2)}) collective-permute-start(bf16[384,512]{1,0:T(8,128)(2,1)S(1)} %copy-done.9), channel_id=1, source_target_pairs={{0,7},{1,0},{2,1},{3,2},{4,3},{5,4},{6,5},{7,6},{8,15},{9,8},{10,9... | collective-permute-start | bytes 1179656 | tf_op jit(solution)/shard_map/ppermute | solution.py:444
  20.4 17.9 %collective-permute-start.11 = (bf16[384,512]{1,0:T(8,128)(2,1)S(1)}, bf16[384,512]{1,0:T(8,128)(2,1)S(1)}, u32[]{:S(2)}, u32[]{:S(2)}) collective-permute-start(bf16[384,512]{1,0:T(8,128)(2,1)S(1)} %copy-done.8), channel_id=1, source_target_pairs={{0,7},{1,0},{2,1},{3,2},{4,3},{5,4},{6,5},{7,6},{8,15},{9,8},{10,9... | collective-permute-start | bytes 1179656 | tf_op jit(solution)/shard_map/ppermute | solution.py:444
  22.3 19.7 %collective-permute-start.1 = (bf16[384,512]{1,0:T(8,128)(2,1)S(1)}, bf16[384,512]{1,0:T(8,128)(2,1)S(1)}, u32[]{:S(2)}, u32[]{:S(2)}) collective-permute-start(bf16[384,512]{1,0:T(8,128)(2,1)S(1)} %copy-done.9), channel_id=1, source_target_pairs={{0,1},{1,2},{2,3},{3,4},{4,5},{5,6},{6,7},{7,0},{8,9},{9,10},{10,1... | collective-permute-start | bytes 1179656 | tf_op jit(solution)/shard_map/ppermute | solution.py:444
  30.2 16.9 %collective-permute-start.2 = (bf16[384,512]{1,0:T(8,128)(2,1)S(1)}, bf16[384,512]{1,0:T(8,128)(2,1)S(1)}, u32[]{:S(2)}, u32[]{:S(2)}) collective-permute-start(bf16[384,512]{1,0:T(8,128)(2,1)S(1)} %collective-permute-done.refs_4_), channel_id=1, source_target_pairs={{0,1},{1,2},{2,3},{3,4},{4,5},{5,6},{6,7},{7,0},{8,9},{9,10},{10,1... | collective-permute-start | bytes 1179656 | tf_op jit(solution)/shard_map/ppermute | solution.py:444
  30.2 16.8 %collective-permute-start.8 = (bf16[384,512]{1,0:T(8,128)(2,1)S(1)}, bf16[384,512]{1,0:T(8,128)(2,1)S(1)}, u32[]{:S(2)}, u32[]{:S(2)}) collective-permute-start(bf16[384,512]{1,0:T(8,128)(2,1)S(1)} %collective-permute-done.7.refs_17_), channel_id=1, source_target_pairs={{0,7},{1,0},{2,1},{3,2},{4,3},{5,4},{6,5},{7,6},{8,15},{9,8},{10,9... | collective-permute-start | bytes 1179656 | tf_op jit(solution)/shard_map/ppermute | solution.py:444
  38.3 16.9 %collective-permute-start.12 = (bf16[384,512]{1,0:T(8,128)(2,1)S(1)}, bf16[384,512]{1,0:T(8,128)(2,1)S(1)}, u32[]{:S(2)}, u32[]{:S(2)}) collective-permute-start(bf16[384,512]{1,0:T(8,128)(2,1)S(1)} %collective-permute-done.11.refs_16_), channel_id=1, source_target_pairs={{0,7},{1,0},{2,1},{3,2},{4,3},{5,4},{6,5},{7,6},{8,15},{9,8},{10,9... | collective-permute-start | bytes 1179656 | tf_op jit(solution)/shard_map/ppermute | solution.py:444
  42.0 16.9 %collective-permute-start.3 = (bf16[384,512]{1,0:T(8,128)(2,1)S(1)}, bf16[384,512]{1,0:T(8,128)(2,1)S(1)}, u32[]{:S(2)}, u32[]{:S(2)}) collective-permute-start(bf16[384,512]{1,0:T(8,128)(2,1)S(1)} %collective-permute-done.1.refs_5_), channel_id=1, source_target_pairs={{0,1},{1,2},{2,3},{3,4},{4,5},{5,6},{6,7},{7,0},{8,9},{9,10},{10,1... | collective-permute-start | bytes 1179656 | tf_op jit(solution)/shard_map/ppermute | solution.py:444
  47.1 16.9 %collective-permute-start.4 = (bf16[384,512]{1,0:T(8,128)(2,1)S(1)}, bf16[384,512]{1,0:T(8,128)(2,1)S(1)}, u32[]{:S(2)}, u32[]{:S(2)}) collective-permute-start(bf16[384,512]{1,0:T(8,128)(2,1)S(1)} %collective-permute-done.2.refs_6_), channel_id=1, source_target_pairs={{0,1},{1,2},{2,3},{3,4},{4,5},{5,6},{6,7},{7,0},{8,9},{9,10},{10,1... | collective-permute-start | bytes 1179656 | tf_op jit(solution)/shard_map/ppermute | solution.py:444
  47.1 16.8 %collective-permute-start.9 = (bf16[384,512]{1,0:T(8,128)(2,1)S(1)}, bf16[384,512]{1,0:T(8,128)(2,1)}, u32[]{:S(2)}, u32[]{:S(2)}) collective-permute-start(bf16[384,512]{1,0:T(8,128)(2,1)S(1)} %collective-permute-done.8.refs_15_), channel_id=1, source_target_pairs={{0,7},{1,0},{2,1},{3,2},{4,3},{5,4},{6,5},{7,6},{8,15},{9,8},{10,9... | collective-permute-start | bytes 1179656 | tf_op jit(solution)/shard_map/ppermute | solution.py:444
  55.2 16.9 %collective-permute-start.13 = (bf16[384,512]{1,0:T(8,128)(2,1)S(1)}, bf16[384,512]{1,0:T(8,128)(2,1)}, u32[]{:S(2)}, u32[]{:S(2)}) collective-permute-start(bf16[384,512]{1,0:T(8,128)(2,1)S(1)} %collective-permute-done.12.refs_14_), channel_id=1, source_target_pairs={{0,7},{1,0},{2,1},{3,2},{4,3},{5,4},{6,5},{7,6},{8,15},{9,8},{10,9... | collective-permute-start | bytes 1179656 | tf_op jit(solution)/shard_map/ppermute | solution.py:444
  58.9 13.6 %collective-permute-start.5 = (bf16[384,512]{1,0:T(8,128)(2,1)S(1)}, bf16[384,512]{1,0:T(8,128)(2,1)}, u32[]{:S(2)}, u32[]{:S(2)}) collective-permute-start(bf16[384,512]{1,0:T(8,128)(2,1)S(1)} %collective-permute-done.3.refs_7_), channel_id=1, source_target_pairs={{0,1},{1,2},{2,3},{3,4},{4,5},{5,6},{6,7},{7,0},{8,9},{9,10},{10,1... | collective-permute-start | bytes 1179656 | tf_op jit(solution)/shard_map/ppermute | solution.py:444
  63.9 16.5 %collective-permute-start.6 = (bf16[384,512]{1,0:T(8,128)(2,1)S(1)}, bf16[384,512]{1,0:T(8,128)(2,1)}, u32[]{:S(2)}, u32[]{:S(2)}) collective-permute-start(bf16[384,512]{1,0:T(8,128)(2,1)S(1)} %collective-permute-done.4.refs_8_), channel_id=1, source_target_pairs={{0,1},{1,2},{2,3},{3,4},{4,5},{5,6},{6,7},{7,0},{8,9},{9,10},{10,1... | collective-permute-start | bytes 1179656 | tf_op jit(solution)/shard_map/ppermute | solution.py:444
  63.9 16.5 %collective-permute-start.10 = (bf16[384,512]{1,0:T(8,128)(2,1)}, bf16[384,512]{1,0:T(8,128)(2,1)}, u32[]{:S(2)}, u32[]{:S(2)}) collective-permute-start(bf16[384,512]{1,0:T(8,128)(2,1)} %collective-permute-done.9.refs_13_), channel_id=1, source_target_pairs={{0,7},{1,0},{2,1},{3,2},{4,3},{5,4},{6,5},{7,6},{8,15},{9,8},{10,9... | collective-permute-start | bytes 1179656 | tf_op jit(solution)/shard_map/ppermute | solution.py:444
  101.9 26.0 %collective-permute-start.14 = (bf16[768,512]{1,0:T(8,128)(2,1)}, bf16[768,512]{1,0:T(8,128)(2,1)}, u32[]{:S(2)}, u32[]{:S(2)}) collective-permute-start(bf16[768,512]{1,0:T(8,128)(2,1)} %get-tuple-element.53), channel_id=1, source_target_pairs={{0,1},{1,2},{2,3},{3,4},{4,5},{5,6},{6,7},{7,0},{8,9},{9,10},{10,1... | collective-permute-start | bytes 2359304 | tf_op jit(solution)/shard_map/ppermute | solution.py:444
  103.9 24.0 %collective-permute-start.15 = (bf16[768,512]{1,0:T(8,128)(2,1)}, bf16[768,512]{1,0:T(8,128)(2,1)}, u32[]{:S(2)}, u32[]{:S(2)}) collective-permute-start(bf16[768,512]{1,0:T(8,128)(2,1)} %get-tuple-element.54), channel_id=1, source_target_pairs={{0,7},{1,0},{2,1},{3,2},{4,3},{5,4},{6,5},{7,6},{8,15},{9,8},{10,9... | collective-permute-start | bytes 2359304 | tf_op jit(solution)/shard_map/ppermute | solution.py:444
  121.0 50.4 %all-to-all-start.1 = ((bf16[32,24,2048]{2,1,0:T(8,128)(2,1)}), bf16[32,24,2048]{2,1,0:T(8,128)(2,1)S(1)}, u32[]{:S(2)}, u32[]{:S(2)}) async-start(bf16[32,24,2048]{2,1,0:T(8,128)(2,1)} %bitcast.11), calls=%async_computation.1 | async-start | bytes 6291456 | tf_op jit(solution)/shard_map/all_to_all | solution.py:490
  133.1 13.5 %collective-permute-start.21 = (bf16[384,512]{1,0:T(8,128)(2,1)S(1)}, bf16[384,512]{1,0:T(8,128)(2,1)S(1)}, u32[]{:S(2)}, u32[]{:S(2)}) collective-permute-start(bf16[384,512]{1,0:T(8,128)(2,1)S(1)} %get-tuple-element.86), channel_id=1, source_target_pairs={{0,1},{1,2},{2,3},{3,4},{4,5},{5,6},{6,7},{7,0},{8,9},{9,10},{10,1... | collective-permute-start | bytes 1179656 | tf_op jit(solution)/shard_map/ppermute | solution.py:444
  133.5 15.8 %collective-permute-start.17 = (bf16[384,512]{1,0:T(8,128)(2,1)S(1)}, bf16[384,512]{1,0:T(8,128)(2,1)S(1)}, u32[]{:S(2)}, u32[]{:S(2)}) collective-permute-start(bf16[384,512]{1,0:T(8,128)(2,1)S(1)} %get-tuple-element.85), channel_id=1, source_target_pairs={{0,7},{1,0},{2,1},{3,2},{4,3},{5,4},{6,5},{7,6},{8,15},{9,8},{10,9... | collective-permute-start | bytes 1179656 | tf_op jit(solution)/shard_map/ppermute | solution.py:444
  136.7 17.3 %collective-permute-start.16 = (bf16[384,512]{1,0:T(8,128)(2,1)S(1)}, bf16[384,512]{1,0:T(8,128)(2,1)S(1)}, u32[]{:S(2)}, u32[]{:S(2)}) collective-permute-start(bf16[384,512]{1,0:T(8,128)(2,1)S(1)} %get-tuple-element.87), channel_id=1, source_target_pairs={{0,1},{1,2},{2,3},{3,4},{4,5},{5,6},{6,7},{7,0},{8,9},{9,10},{10,1... | collective-permute-start | bytes 1179656 | tf_op jit(solution)/shard_map/ppermute | solution.py:444
  154.3 13.3 %collective-permute-start.18 = (bf16[384,512]{1,0:T(8,128)(2,1)S(1)}, bf16[384,512]{1,0:T(8,128)(2,1)S(1)}, u32[]{:S(2)}, u32[]{:S(2)}) collective-permute-start(bf16[384,512]{1,0:T(8,128)(2,1)S(1)} %add_convert_fusion.7), channel_id=1, source_target_pairs={{0,1},{1,2},{2,3},{3,4},{4,5},{5,6},{6,7},{7,0},{8,9},{9,10},{10,1... | collective-permute-start | bytes 1179656 | tf_op jit(solution)/shard_map/ppermute | solution.py:444
  157.2 18.8 %collective-permute-start.24 = (bf16[384,512]{1,0:T(8,128)(2,1)}, bf16[384,512]{1,0:T(8,128)(2,1)S(1)}, u32[]{:S(2)}, u32[]{:S(2)}) collective-permute-start(bf16[384,512]{1,0:T(8,128)(2,1)} %add_convert_fusion.1), channel_id=1, source_target_pairs={{0,1},{1,2},{2,3},{3,4},{4,5},{5,6},{6,7},{7,0},{8,9},{9,10},{10,1... | collective-permute-start | bytes 1179656 | tf_op jit(solution)/shard_map/ppermute | solution.py:444
  158.1 17.9 %collective-permute-start.23 = (bf16[384,512]{1,0:T(8,128)(2,1)}, bf16[384,512]{1,0:T(8,128)(2,1)}, u32[]{:S(2)}, u32[]{:S(2)}) collective-permute-start(bf16[384,512]{1,0:T(8,128)(2,1)} %add_convert_fusion.2), channel_id=1, source_target_pairs={{0,7},{1,0},{2,1},{3,2},{4,3},{5,4},{6,5},{7,6},{8,15},{9,8},{10,9... | collective-permute-start | bytes 1179656 | tf_op jit(solution)/shard_map/ppermute | solution.py:444
  (24 other events, 675.3 us)

commit v3 on v2

--- a/solution.py
+++ b/solution.py
@@ -358,9 +358,8 @@
         cols = (slice(None), pl.ds(pl.multiple_of(i * TERM_COLS, TERM_COLS), TERM_COLS))
         return pltpu.make_async_copy(row_grad.at[cols], row_grad_hbm.at[cols], row_sems.at[i])
 
-    @pl.loop(0, width // TERM_COLS)
-    def _(i):
-        span = pl.ds(pl.multiple_of(i * TERM_COLS, TERM_COLS), TERM_COLS)
+    for i in range(width // TERM_COLS):
+        span = slice(i * TERM_COLS, (i + 1) * TERM_COLS)
         value = matmul(grads[:, :ff], w[0, span, :], ((1,), (1,)))
         value = value + matmul(grads[:, ff:], w[1, span, :], ((1,), (1,)))
         row_grad[:, span] = value.astype(jnp.bfloat16)

time: 186 us -> 185 us (level)
  no operation moved by 1% of the time
where the time goes in v3:
time: 185 us
  waiting for transfers between devices  81.5 us (44%)
  starting transfers between devices  59.3 us (32%)
  Pallas kernels  33.2 us (18%)
  other arithmetic  6.76 us (4%)
  matrix products  2.76 us (1%)
    ppermute x26, waiting for transfers between devices, shift(): return lax.ppermute(a, 'dp', [(i, (i + by) % n) for i in range(n)])  72.4 us
    ppermute x26, starting transfers between devices, shift(): return lax.ppermute(a, 'dp', [(i, (i + by) % n) for i in range(n)])  44.4 us
    all_to_all x2, starting transfers between devices, exchange(): lax.all_to_all(rows.reshape(experts, capacity, rows.shape[1]), 'expert',...  14.9 us
    pallas_call x1, Pallas kernels, terms_of(): pl.pallas_call(lambda *refs: rest_kernel(parts, *refs), in_specs=[pl.Bloc...  12.5 us
    pallas_call x1, Pallas kernels, terms_of(): pl.pallas_call(lambda *refs: terms_kernel(parts, *refs), in_specs=[pl.Blo...  12.3 us
    all_to_all x2, waiting for transfers between devices, exchange(): lax.all_to_all(rows.reshape(experts, capacity, rows.shape[1]), 'expert',...  9.14 us
    convert_element_type x8, other arithmetic, ring_scatter(): arrived[c, by] = shift(total.astype(jnp.bfloat16), by)  6.76 us
    pallas_call x1, Pallas kernels, pack(): pl.pallas_call(lambda *refs: pack_kernel(capacity, *refs), in_specs=[vmem...  5.88 us
  transfers between devices with their start and end apart: 28, of which 18 were waited for; matrix products, arithmetic and copies ran while one was open for 5% of the time, Pallas kernels for 7%

profile of v3, /device:TPU:2, one launch (start us, length us, event | category | flops | bytes accessed | tf_op | source)
XLA Modules:
  0.0 184.6 jit_solution(10903227419008394215)
XLA Ops:
  0.6 5.9 %pack.1 = (bf16[768,4096]{1,0:T(8,128)(2,1)}, s32[32,128]{1,0:T(8,128)}, bf16[384,512]{1,0:T(8,128)(2,1)}, bf16[384,512]{1,0:T(8,128)(2,1)}) custom-call(s32[4,128]{1,0:T(4,128)} %bitcast.12, bf16[4,128]{1,0:T(4,128)(2,1)} %bitcast.13, bf16[128,2048]{1,0:T(8,128)(2,1)} %refs_2_.1, bf16[128,2048]{1,0:T(8,128)(2,1)} %refs_3_.1, bf16[1,256,512]{2,1,0:T(8,128)(2,1)} %refs_4_.1, ...), custom_call_target="tpu_custom_call" | custom-call | flops 805306368 | bytes 6291456 | tf_op jit(solution)/shard_map/pack/pallas_call | solution.py:124
  6.5 7.8 %all-to-all-start = ((bf16[32,24,4096]{2,1,0:T(8,128)(2,1)}), bf16[32,24,4096]{2,1,0:T(8,128)(2,1)}, u32[]{:S(2)}, u32[]{:S(2)}) async-start(bf16[32,24,4096]{2,1,0:T(8,128)(2,1)} %bitcast.10), calls=%async_computation | async-start | bytes 12582912 | tf_op jit(solution)/shard_map/all_to_all | solution.py:489
  16.4 4.0 %collective-permute-start.7 = (bf16[384,512]{1,0:T(8,128)(2,1)S(1)}, bf16[384,512]{1,0:T(8,128)(2,1)S(1)}, u32[]{:S(2)}, u32[]{:S(2)}) collective-permute-start(bf16[384,512]{1,0:T(8,128)(2,1)S(1)} %copy-done.9), channel_id=1, source_target_pairs={{0,7},{1,0},{2,1},{3,2},{4,3},{5,4},{6,5},{7,6},{8,15},{9,8},{10,9... | collective-permute-start | bytes 1179656 | tf_op jit(solution)/shard_map/ppermute | solution.py:443
  22.4 7.8 %collective-permute-done.refs_4_ = bf16[384,512]{1,0:T(8,128)(2,1)S(1)} collective-permute-done((bf16[384,512]{1,0:T(8,128)(2,1)S(1)}, bf16[384,512]{1,0:T(8,128)(2,1)S(1)}, u32[]{:S(2)}, u32[]{:S(2)}) %collective-permute-start) | collective-permute-done | bytes 393248 | tf_op jit(solution)/shard_map/ppermute | solution.py:443
  30.2 3.4 %collective-permute-start.8 = (bf16[384,512]{1,0:T(8,128)(2,1)S(1)}, bf16[384,512]{1,0:T(8,128)(2,1)S(1)}, u32[]{:S(2)}, u32[]{:S(2)}) collective-permute-start(bf16[384,512]{1,0:T(8,128)(2,1)S(1)} %collective-permute-done.7.refs_17_), channel_id=1, source_target_pairs={{0,7},{1,0},{2,1},{3,2},{4,3},{5,4},{6,5},{7,6},{8,15},{9,8},{10,9... | collective-permute-start | bytes 1179656 | tf_op jit(solution)/shard_map/ppermute | solution.py:443
  33.6 4.7 %collective-permute-done.11.refs_16_ = bf16[384,512]{1,0:T(8,128)(2,1)S(1)} collective-permute-done((bf16[384,512]{1,0:T(8,128)(2,1)S(1)}, bf16[384,512]{1,0:T(8,128)(2,1)S(1)}, u32[]{:S(2)}, u32[]{:S(2)}) %collective-permute-start.11) | collective-permute-done | bytes 393248 | tf_op jit(solution)/shard_map/ppermute | solution.py:443
  38.3 3.7 %collective-permute-start.12 = (bf16[384,512]{1,0:T(8,128)(2,1)S(1)}, bf16[384,512]{1,0:T(8,128)(2,1)S(1)}, u32[]{:S(2)}, u32[]{:S(2)}) collective-permute-start(bf16[384,512]{1,0:T(8,128)(2,1)S(1)} %collective-permute-done.11.refs_16_), channel_id=1, source_target_pairs={{0,7},{1,0},{2,1},{3,2},{4,3},{5,4},{6,5},{7,6},{8,15},{9,8},{10,9... | collective-permute-start | bytes 1179656 | tf_op jit(solution)/shard_map/ppermute | solution.py:443
  42.0 5.0 %collective-permute-done.2.refs_6_ = bf16[384,512]{1,0:T(8,128)(2,1)S(1)} collective-permute-done((bf16[384,512]{1,0:T(8,128)(2,1)S(1)}, bf16[384,512]{1,0:T(8,128)(2,1)S(1)}, u32[]{:S(2)}, u32[]{:S(2)}) %collective-permute-start.2) | collective-permute-done | bytes 393248 | tf_op jit(solution)/shard_map/ppermute | solution.py:443
  50.4 4.7 %collective-permute-done.12.refs_14_ = bf16[384,512]{1,0:T(8,128)(2,1)S(1)} collective-permute-done((bf16[384,512]{1,0:T(8,128)(2,1)S(1)}, bf16[384,512]{1,0:T(8,128)(2,1)S(1)}, u32[]{:S(2)}, u32[]{:S(2)}) %collective-permute-start.12) | collective-permute-done | bytes 393248 | tf_op jit(solution)/shard_map/ppermute | solution.py:443
  55.2 3.7 %collective-permute-start.13 = (bf16[384,512]{1,0:T(8,128)(2,1)S(1)}, bf16[384,512]{1,0:T(8,128)(2,1)}, u32[]{:S(2)}, u32[]{:S(2)}) collective-permute-start(bf16[384,512]{1,0:T(8,128)(2,1)S(1)} %collective-permute-done.12.refs_14_), channel_id=1, source_target_pairs={{0,7},{1,0},{2,1},{3,2},{4,3},{5,4},{6,5},{7,6},{8,15},{9,8},{10,9... | collective-permute-start | bytes 1179656 | tf_op jit(solution)/shard_map/ppermute | solution.py:443
  58.9 5.0 %collective-permute-done.4.refs_8_ = bf16[384,512]{1,0:T(8,128)(2,1)S(1)} collective-permute-done((bf16[384,512]{1,0:T(8,128)(2,1)S(1)}, bf16[384,512]{1,0:T(8,128)(2,1)S(1)}, u32[]{:S(2)}, u32[]{:S(2)}) %collective-permute-start.4) | collective-permute-done | bytes 393248 | tf_op jit(solution)/shard_map/ppermute | solution.py:443
  63.9 3.5 %collective-permute-start.10 = (bf16[384,512]{1,0:T(8,128)(2,1)}, bf16[384,512]{1,0:T(8,128)(2,1)}, u32[]{:S(2)}, u32[]{:S(2)}) collective-permute-start(bf16[384,512]{1,0:T(8,128)(2,1)} %collective-permute-done.9.refs_13_), channel_id=1, source_target_pairs={{0,7},{1,0},{2,1},{3,2},{4,3},{5,4},{6,5},{7,6},{8,15},{9,8},{10,9... | collective-permute-start | bytes 1179656 | tf_op jit(solution)/shard_map/ppermute | solution.py:443
  67.4 4.6 %collective-permute-done.13.refs_12_ = bf16[384,512]{1,0:T(8,128)(2,1)} collective-permute-done((bf16[384,512]{1,0:T(8,128)(2,1)S(1)}, bf16[384,512]{1,0:T(8,128)(2,1)}, u32[]{:S(2)}, u32[]{:S(2)}) %collective-permute-start.13) | collective-permute-done | bytes 393248 | tf_op jit(solution)/shard_map/ppermute | solution.py:443
  72.4 8.0 %collective-permute-done.6.refs_10_ = bf16[384,512]{1,0:T(8,128)(2,1)} collective-permute-done((bf16[384,512]{1,0:T(8,128)(2,1)S(1)}, bf16[384,512]{1,0:T(8,128)(2,1)}, u32[]{:S(2)}, u32[]{:S(2)}) %collective-permute-start.6) | collective-permute-done | bytes 393248 | tf_op jit(solution)/shard_map/ppermute | solution.py:443
  80.4 9.1 %all-to-all-done = bf16[32,24,4096]{2,1,0:T(8,128)(2,1)} async-done(((bf16[32,24,4096]{2,1,0:T(8,128)(2,1)}), bf16[32,24,4096]{2,1,0:T(8,128)(2,1)}, u32[]{:S(2)}, u32[]{:S(2)}) %all-to-all-start) | async-done | bytes 6291488 | tf_op jit(solution)/shard_map/all_to_all | solution.py:489
  89.6 12.3 %terms.1 = (bf16[768,1024]{1,0:T(8,128)(2,1)}, bf16[512,768]{1,0:T(8,128)(2,1)}, bf16[2,2048,512]{2,1,0:T(8,128)(2,1)}, bf16[768,512]{1,0:T(8,128)(2,1)}, bf16[768,512]{1,0:T(8,128)(2,1)}) custom-call(s32[1]{0:T(128)} %bitcast.2.refs_0_, bf16[768,4096]{1,0:T(8,128)(2,1)} %bitcast.4.refs_1_, bf16[384,512]{1,0:T(8,128)(2,1)} %get-tuple-element.46.refs_2_, ...), custom_call_target="tpu_custom_call" | custom-call | flops 6442450944 | bytes 18874368 | tf_op jit(solution)/shard_map/terms/pallas_call | solution.py:282
  103.9 4.0 %collective-permute-start.15 = (bf16[768,512]{1,0:T(8,128)(2,1)}, bf16[768,512]{1,0:T(8,128)(2,1)}, u32[]{:S(2)}, u32[]{:S(2)}) collective-permute-start(bf16[768,512]{1,0:T(8,128)(2,1)} %get-tuple-element.54), channel_id=1, source_target_pairs={{0,7},{1,0},{2,1},{3,2},{4,3},{5,4},{6,5},{7,6},{8,15},{9,8},{10,9... | collective-permute-start | bytes 2359304 | tf_op jit(solution)/shard_map/ppermute | solution.py:443
  107.9 12.5 %rest.1 = (bf16[768,2048]{1,0:T(8,128)(2,1)}, bf16[384,512]{1,0:T(8,128)(2,1)}, bf16[384,512]{1,0:T(8,128)(2,1)}, bf16[384,512]{1,0:T(8,128)(2,1)}, bf16[384,512...) custom-call(s32[1]{0:T(128)} %bitcast.2.refs_0_, ...), custom_call_target="tpu_custom_call" | custom-call | flops 6442450944 | bytes 19922944 | tf_op jit(solution)/shard_map/rest/pallas_call | solution.py:311
  120.4 7.1 %all-to-all-start.1 = ((bf16[32,24,2048]{2,1,0:T(8,128)(2,1)}), bf16[32,24,2048]{2,1,0:T(8,128)(2,1)S(1)}, u32[]{:S(2)}, u32[]{:S(2)}) async-start(bf16[32,24,2048]{2,1,0:T(8,128)(2,1)} %bitcast.11), calls=%async_computation.1 | async-start | bytes 6291456 | tf_op jit(solution)/shard_map/all_to_all | solution.py:489
  136.1 5.2 %collective-permute-done.22 = bf16[384,512]{1,0:T(8,128)(2,1)S(1)} collective-permute-done((bf16[384,512]{1,0:T(8,128)(2,1)S(1)}, bf16[384,512]{1,0:T(8,128)(2,1)S(1)}, u32[]{:S(2)}, u32[]{:S(2)}) %collective-permute-start.22) | collective-permute-done | bytes 393248 | tf_op jit(solution)/shard_map/ppermute | solution.py:443
  141.2 4.8 %collective-permute-done.21 = bf16[384,512]{1,0:T(8,128)(2,1)S(1)} collective-permute-done((bf16[384,512]{1,0:T(8,128)(2,1)S(1)}, bf16[384,512]{1,0:T(8,128)(2,1)S(1)}, u32[]{:S(2)}, u32[]{:S(2)}) %collective-permute-start.21) | collective-permute-done | bytes 393248 | tf_op jit(solution)/shard_map/ppermute | solution.py:443
  148.9 4.5 %collective-permute-done.16 = bf16[384,512]{1,0:T(8,128)(2,1)S(1)} collective-permute-done((bf16[384,512]{1,0:T(8,128)(2,1)S(1)}, bf16[384,512]{1,0:T(8,128)(2,1)S(1)}, u32[]{:S(2)}, u32[]{:S(2)}) %collective-permute-start.16) | collective-permute-done | bytes 393248 | tf_op jit(solution)/shard_map/ppermute | solution.py:443
  160.7 4.9 %collective-permute-done.19 = bf16[384,512]{1,0:T(8,128)(2,1)S(1)} collective-permute-done((bf16[384,512]{1,0:T(8,128)(2,1)S(1)}, bf16[384,512]{1,0:T(8,128)(2,1)S(1)}, u32[]{:S(2)}, u32[]{:S(2)}) %collective-permute-start.19) | collective-permute-done | bytes 393248 | tf_op jit(solution)/shard_map/ppermute | solution.py:443
  175.4 5.1 %collective-permute-done.25.left_b = bf16[384,512]{1,0:T(8,128)(2,1)} collective-permute-done((bf16[384,512]{1,0:T(8,128)(2,1)}, bf16[384,512]{1,0:T(8,128)(2,1)}, u32[]{:S(2)}, u32[]{:S(2)}) %collective-permute-start.25) | collective-permute-done | bytes 393248 | tf_op jit(solution)/shard_map/ppermute | solution.py:443
  (85 shorter events, 42.4 us)
Async XLA Ops:
  6.5 83.0 %all-to-all-start = ((bf16[32,24,4096]{2,1,0:T(8,128)(2,1)}), bf16[32,24,4096]{2,1,0:T(8,128)(2,1)}, u32[]{:S(2)}, u32[]{:S(2)}) async-start(bf16[32,24,4096]{2,1,0:T(8,128)(2,1)} %bitcast.10), calls=%async_computation | async-start | bytes 12582912 | tf_op jit(solution)/shard_map/all_to_all | solution.py:489
  14.4 15.8 %collective-permute-start = (bf16[384,512]{1,0:T(8,128)(2,1)S(1)}, bf16[384,512]{1,0:T(8,128)(2,1)S(1)}, u32[]{:S(2)}, u32[]{:S(2)}) collective-permute-start(bf16[384,512]{1,0:T(8,128)(2,1)S(1)} %copy-done.8), channel_id=1, source_target_pairs={{0,1},{1,2},{2,3},{3,4},{4,5},{5,6},{6,7},{7,0},{8,9},{9,10},{10,1... | collective-permute-start | bytes 1179656 | tf_op jit(solution)/shard_map/ppermute | solution.py:443
  16.4 13.8 %collective-permute-start.7 = (bf16[384,512]{1,0:T(8,128)(2,1)S(1)}, bf16[384,512]{1,0:T(8,128)(2,1)S(1)}, u32[]{:S(2)}, u32[]{:S(2)}) collective-permute-start(bf16[384,512]{1,0:T(8,128)(2,1)S(1)} %copy-done.9), channel_id=1, source_target_pairs={{0,7},{1,0},{2,1},{3,2},{4,3},{5,4},{6,5},{7,6},{8,15},{9,8},{10,9... | collective-permute-start | bytes 1179656 | tf_op jit(solution)/shard_map/ppermute | solution.py:443
  20.4 17.9 %collective-permute-start.11 = (bf16[384,512]{1,0:T(8,128)(2,1)S(1)}, bf16[384,512]{1,0:T(8,128)(2,1)S(1)}, u32[]{:S(2)}, u32[]{:S(2)}) collective-permute-start(bf16[384,512]{1,0:T(8,128)(2,1)S(1)} %copy-done.8), channel_id=1, source_target_pairs={{0,7},{1,0},{2,1},{3,2},{4,3},{5,4},{6,5},{7,6},{8,15},{9,8},{10,9... | collective-permute-start | bytes 1179656 | tf_op jit(solution)/shard_map/ppermute | solution.py:443
  22.3 19.7 %collective-permute-start.1 = (bf16[384,512]{1,0:T(8,128)(2,1)S(1)}, bf16[384,512]{1,0:T(8,128)(2,1)S(1)}, u32[]{:S(2)}, u32[]{:S(2)}) collective-permute-start(bf16[384,512]{1,0:T(8,128)(2,1)S(1)} %copy-done.9), channel_id=1, source_target_pairs={{0,1},{1,2},{2,3},{3,4},{4,5},{5,6},{6,7},{7,0},{8,9},{9,10},{10,1... | collective-permute-start | bytes 1179656 | tf_op jit(solution)/shard_map/ppermute | solution.py:443
  30.2 16.9 %collective-permute-start.2 = (bf16[384,512]{1,0:T(8,128)(2,1)S(1)}, bf16[384,512]{1,0:T(8,128)(2,1)S(1)}, u32[]{:S(2)}, u32[]{:S(2)}) collective-permute-start(bf16[384,512]{1,0:T(8,128)(2,1)S(1)} %collective-permute-done.refs_4_), channel_id=1, source_target_pairs={{0,1},{1,2},{2,3},{3,4},{4,5},{5,6},{6,7},{7,0},{8,9},{9,10},{10,1... | collective-permute-start | bytes 1179656 | tf_op jit(solution)/shard_map/ppermute | solution.py:443
  30.2 16.8 %collective-permute-start.8 = (bf16[384,512]{1,0:T(8,128)(2,1)S(1)}, bf16[384,512]{1,0:T(8,128)(2,1)S(1)}, u32[]{:S(2)}, u32[]{:S(2)}) collective-permute-start(bf16[384,512]{1,0:T(8,128)(2,1)S(1)} %collective-permute-done.7.refs_17_), channel_id=1, source_target_pairs={{0,7},{1,0},{2,1},{3,2},{4,3},{5,4},{6,5},{7,6},{8,15},{9,8},{10,9... | collective-permute-start | bytes 1179656 | tf_op jit(solution)/shard_map/ppermute | solution.py:443
  38.3 16.9 %collective-permute-start.12 = (bf16[384,512]{1,0:T(8,128)(2,1)S(1)}, bf16[384,512]{1,0:T(8,128)(2,1)S(1)}, u32[]{:S(2)}, u32[]{:S(2)}) collective-permute-start(bf16[384,512]{1,0:T(8,128)(2,1)S(1)} %collective-permute-done.11.refs_16_), channel_id=1, source_target_pairs={{0,7},{1,0},{2,1},{3,2},{4,3},{5,4},{6,5},{7,6},{8,15},{9,8},{10,9... | collective-permute-start | bytes 1179656 | tf_op jit(solution)/shard_map/ppermute | solution.py:443
  42.0 16.9 %collective-permute-start.3 = (bf16[384,512]{1,0:T(8,128)(2,1)S(1)}, bf16[384,512]{1,0:T(8,128)(2,1)S(1)}, u32[]{:S(2)}, u32[]{:S(2)}) collective-permute-start(bf16[384,512]{1,0:T(8,128)(2,1)S(1)} %collective-permute-done.1.refs_5_), channel_id=1, source_target_pairs={{0,1},{1,2},{2,3},{3,4},{4,5},{5,6},{6,7},{7,0},{8,9},{9,10},{10,1... | collective-permute-start | bytes 1179656 | tf_op jit(solution)/shard_map/ppermute | solution.py:443
  47.1 16.9 %collective-permute-start.4 = (bf16[384,512]{1,0:T(8,128)(2,1)S(1)}, bf16[384,512]{1,0:T(8,128)(2,1)S(1)}, u32[]{:S(2)}, u32[]{:S(2)}) collective-permute-start(bf16[384,512]{1,0:T(8,128)(2,1)S(1)} %collective-permute-done.2.refs_6_), channel_id=1, source_target_pairs={{0,1},{1,2},{2,3},{3,4},{4,5},{5,6},{6,7},{7,0},{8,9},{9,10},{10,1... | collective-permute-start | bytes 1179656 | tf_op jit(solution)/shard_map/ppermute | solution.py:443
  47.1 16.8 %collective-permute-start.9 = (bf16[384,512]{1,0:T(8,128)(2,1)S(1)}, bf16[384,512]{1,0:T(8,128)(2,1)}, u32[]{:S(2)}, u32[]{:S(2)}) collective-permute-start(bf16[384,512]{1,0:T(8,128)(2,1)S(1)} %collective-permute-done.8.refs_15_), channel_id=1, source_target_pairs={{0,7},{1,0},{2,1},{3,2},{4,3},{5,4},{6,5},{7,6},{8,15},{9,8},{10,9... | collective-permute-start | bytes 1179656 | tf_op jit(solution)/shard_map/ppermute | solution.py:443
  55.2 16.9 %collective-permute-start.13 = (bf16[384,512]{1,0:T(8,128)(2,1)S(1)}, bf16[384,512]{1,0:T(8,128)(2,1)}, u32[]{:S(2)}, u32[]{:S(2)}) collective-permute-start(bf16[384,512]{1,0:T(8,128)(2,1)S(1)} %collective-permute-done.12.refs_14_), channel_id=1, source_target_pairs={{0,7},{1,0},{2,1},{3,2},{4,3},{5,4},{6,5},{7,6},{8,15},{9,8},{10,9... | collective-permute-start | bytes 1179656 | tf_op jit(solution)/shard_map/ppermute | solution.py:443
  58.9 13.6 %collective-permute-start.5 = (bf16[384,512]{1,0:T(8,128)(2,1)S(1)}, bf16[384,512]{1,0:T(8,128)(2,1)}, u32[]{:S(2)}, u32[]{:S(2)}) collective-permute-start(bf16[384,512]{1,0:T(8,128)(2,1)S(1)} %collective-permute-done.3.refs_7_), channel_id=1, source_target_pairs={{0,1},{1,2},{2,3},{3,4},{4,5},{5,6},{6,7},{7,0},{8,9},{9,10},{10,1... | collective-permute-start | bytes 1179656 | tf_op jit(solution)/shard_map/ppermute | solution.py:443
  63.9 16.5 %collective-permute-start.6 = (bf16[384,512]{1,0:T(8,128)(2,1)S(1)}, bf16[384,512]{1,0:T(8,128)(2,1)}, u32[]{:S(2)}, u32[]{:S(2)}) collective-permute-start(bf16[384,512]{1,0:T(8,128)(2,1)S(1)} %collective-permute-done.4.refs_8_), channel_id=1, source_target_pairs={{0,1},{1,2},{2,3},{3,4},{4,5},{5,6},{6,7},{7,0},{8,9},{9,10},{10,1... | collective-permute-start | bytes 1179656 | tf_op jit(solution)/shard_map/ppermute | solution.py:443
  63.9 16.5 %collective-permute-start.10 = (bf16[384,512]{1,0:T(8,128)(2,1)}, bf16[384,512]{1,0:T(8,128)(2,1)}, u32[]{:S(2)}, u32[]{:S(2)}) collective-permute-start(bf16[384,512]{1,0:T(8,128)(2,1)} %collective-permute-done.9.refs_13_), channel_id=1, source_target_pairs={{0,7},{1,0},{2,1},{3,2},{4,3},{5,4},{6,5},{7,6},{8,15},{9,8},{10,9... | collective-permute-start | bytes 1179656 | tf_op jit(solution)/shard_map/ppermute | solution.py:443
  101.9 25.6 %collective-permute-start.14 = (bf16[768,512]{1,0:T(8,128)(2,1)}, bf16[768,512]{1,0:T(8,128)(2,1)}, u32[]{:S(2)}, u32[]{:S(2)}) collective-permute-start(bf16[768,512]{1,0:T(8,128)(2,1)} %get-tuple-element.53), channel_id=1, source_target_pairs={{0,1},{1,2},{2,3},{3,4},{4,5},{5,6},{6,7},{7,0},{8,9},{9,10},{10,1... | collective-permute-start | bytes 2359304 | tf_op jit(solution)/shard_map/ppermute | solution.py:443
  103.9 23.6 %collective-permute-start.15 = (bf16[768,512]{1,0:T(8,128)(2,1)}, bf16[768,512]{1,0:T(8,128)(2,1)}, u32[]{:S(2)}, u32[]{:S(2)}) collective-permute-start(bf16[768,512]{1,0:T(8,128)(2,1)} %get-tuple-element.54), channel_id=1, source_target_pairs={{0,7},{1,0},{2,1},{3,2},{4,3},{5,4},{6,5},{7,6},{8,15},{9,8},{10,9... | collective-permute-start | bytes 2359304 | tf_op jit(solution)/shard_map/ppermute | solution.py:443
  120.4 50.3 %all-to-all-start.1 = ((bf16[32,24,2048]{2,1,0:T(8,128)(2,1)}), bf16[32,24,2048]{2,1,0:T(8,128)(2,1)S(1)}, u32[]{:S(2)}, u32[]{:S(2)}) async-start(bf16[32,24,2048]{2,1,0:T(8,128)(2,1)} %bitcast.11), calls=%async_computation.1 | async-start | bytes 6291456 | tf_op jit(solution)/shard_map/all_to_all | solution.py:489
  132.7 13.3 %collective-permute-start.21 = (bf16[384,512]{1,0:T(8,128)(2,1)S(1)}, bf16[384,512]{1,0:T(8,128)(2,1)S(1)}, u32[]{:S(2)}, u32[]{:S(2)}) collective-permute-start(bf16[384,512]{1,0:T(8,128)(2,1)S(1)} %get-tuple-element.86), channel_id=1, source_target_pairs={{0,1},{1,2},{2,3},{3,4},{4,5},{5,6},{6,7},{7,0},{8,9},{9,10},{10,1... | collective-permute-start | bytes 1179656 | tf_op jit(solution)/shard_map/ppermute | solution.py:443
  132.9 16.0 %collective-permute-start.17 = (bf16[384,512]{1,0:T(8,128)(2,1)S(1)}, bf16[384,512]{1,0:T(8,128)(2,1)S(1)}, u32[]{:S(2)}, u32[]{:S(2)}) collective-permute-start(bf16[384,512]{1,0:T(8,128)(2,1)S(1)} %get-tuple-element.85), channel_id=1, source_target_pairs={{0,7},{1,0},{2,1},{3,2},{4,3},{5,4},{6,5},{7,6},{8,15},{9,8},{10,9... | collective-permute-start | bytes 1179656 | tf_op jit(solution)/shard_map/ppermute | solution.py:443
  136.1 17.3 %collective-permute-start.16 = (bf16[384,512]{1,0:T(8,128)(2,1)S(1)}, bf16[384,512]{1,0:T(8,128)(2,1)S(1)}, u32[]{:S(2)}, u32[]{:S(2)}) collective-permute-start(bf16[384,512]{1,0:T(8,128)(2,1)S(1)} %get-tuple-element.87), channel_id=1, source_target_pairs={{0,1},{1,2},{2,3},{3,4},{4,5},{5,6},{6,7},{7,0},{8,9},{9,10},{10,1... | collective-permute-start | bytes 1179656 | tf_op jit(solution)/shard_map/ppermute | solution.py:443
  153.7 13.3 %collective-permute-start.18 = (bf16[384,512]{1,0:T(8,128)(2,1)S(1)}, bf16[384,512]{1,0:T(8,128)(2,1)S(1)}, u32[]{:S(2)}, u32[]{:S(2)}) collective-permute-start(bf16[384,512]{1,0:T(8,128)(2,1)S(1)} %add_convert_fusion.7), channel_id=1, source_target_pairs={{0,1},{1,2},{2,3},{3,4},{4,5},{5,6},{6,7},{7,0},{8,9},{9,10},{10,1... | collective-permute-start | bytes 1179656 | tf_op jit(solution)/shard_map/ppermute | solution.py:443
  156.6 18.8 %collective-permute-start.24 = (bf16[384,512]{1,0:T(8,128)(2,1)}, bf16[384,512]{1,0:T(8,128)(2,1)S(1)}, u32[]{:S(2)}, u32[]{:S(2)}) collective-permute-start(bf16[384,512]{1,0:T(8,128)(2,1)} %add_convert_fusion.1), channel_id=1, source_target_pairs={{0,1},{1,2},{2,3},{3,4},{4,5},{5,6},{6,7},{7,0},{8,9},{9,10},{10,1... | collective-permute-start | bytes 1179656 | tf_op jit(solution)/shard_map/ppermute | solution.py:443
  157.5 17.9 %collective-permute-start.23 = (bf16[384,512]{1,0:T(8,128)(2,1)}, bf16[384,512]{1,0:T(8,128)(2,1)}, u32[]{:S(2)}, u32[]{:S(2)}) collective-permute-start(bf16[384,512]{1,0:T(8,128)(2,1)} %add_convert_fusion.2), channel_id=1, source_target_pairs={{0,7},{1,0},{2,1},{3,2},{4,3},{5,4},{6,5},{7,6},{8,15},{9,8},{10,9... | collective-permute-start | bytes 1179656 | tf_op jit(solution)/shard_map/ppermute | solution.py:443
  (24 other events, 674.1 us)
